TPU v7x, 256 devices: a whole 4x4x8 slice. The times are simulated.
256 devices in a mesh: pipe: 8 (over z_lo, core), expert: 32 (over x, y, z_hi).
Axes of the slice: x: 4, y: 4, z: 8 (z_hi: 2, z_lo: 4; z = z_hi * 4 + z_lo), core: 2. Of those that a mesh axis runs over, the one named last changes fastest.
Arguments:
- a_input: bfloat16 [8, 4096, 3584], P('pipe', 'expert'), may hold values from -6 to 6
- a_route: int32 [8, 4096, 1], P('pipe', 'expert'), may hold values from 0 to 7; in each aligned block of 128 rows (0 to 127, 128 to 255, ..., all dimensions but the last counted through in order) at most 18 rows name the same one
- b_saved: bfloat16 [8, 4096, 3584], P('pipe', 'expert'), may hold values from -6 to 6
- b_grad: bfloat16 [8, 4096, 3584], P('pipe', 'expert'), may hold values from -6 to 6
- b_route: int32 [8, 4096, 1], P('pipe', 'expert'), may hold values from 0 to 7; in each aligned block of 128 rows (0 to 127, 128 to 255, ..., all dimensions but the last counted through in order) at most 18 rows name the same one
- up_weight: bfloat16 [8, 3584, 8192], P('pipe', None, 'expert'), may hold values from -0.09375 to 0.09375
- down_weight: bfloat16 [8, 8192, 3584], P('pipe', 'expert'), may hold values from -0.1875 to 0.1875
- router: bfloat16 [8, 3584, 8], P('pipe'), may hold values from -0.09375 to 0.09375
Outputs:
- a_next: bfloat16 [8, 4096, 3584], P('pipe', 'expert')
- b_next: bfloat16 [8, 4096, 3584], P('pipe', 'expert')
- up_grad: bfloat16 [8, 3584, 8192], P('pipe', None, 'expert')
- down_grad: bfloat16 [8, 8192, 3584], P('pipe', 'expert')
Inputs may be any that keep to these rules, and one draw needn't show every extreme that they name: `a_route`: within each device's 128 rows, no expert is named by more than 18 of the (token, choice) pairs, a bound that some block reaches. `b_route`: within each device's 128 rows, no expert is named by more than 18 of the (token, choice) pairs, a bound that some block reaches.
All inputs are finite; a program needn't handle non-finite values.
Results may differ from a plain program's by a relative error of at most 0.0067.
Values may be sent and summed in bfloat16 or wider, within the bound.
A program may use at most 128 MiB of HBM per device.

v0:
```python
import jax
import jax.numpy as jnp
from jax import lax
from jax.sharding import PartitionSpec as P

EPS = 1e-06


def partner(block, axis, bit):
    count = lax.axis_size(axis)
    route = []
    for low in range(count):
        high = low | 1 << bit
        if high != low and high < count:
            route += [(low, high), (high, low)]
    return lax.ppermute(block, axis, route)


def from_behind(array, axis, by):
    devices = lax.axis_size(axis)
    return lax.ppermute(array, axis, [(i, (i + by) % devices) for i in range(devices)])


def rounded(values):
    return lax.optimization_barrier(values.astype(jnp.bfloat16)).astype(jnp.float32)


def route_plan(features, route_ids, router_cols, capacity):
    feat_float = features.astype(jnp.float32)
    inv_scale = lax.rsqrt(jnp.mean(feat_float * feat_float, axis=-1, keepdims=True) + EPS)
    normed = (feat_float * inv_scale).astype(jnp.bfloat16)
    scores = jnp.dot(normed, router_cols, preferred_element_type=jnp.float32)
    gate_value = jax.nn.sigmoid(jnp.take_along_axis(scores, route_ids, axis=1))
    flat_ids = route_ids.reshape(-1)
    onehot = (flat_ids[:, None] == jnp.arange(router_cols.shape[1], dtype=jnp.int32)).astype(
        jnp.int32
    )
    slot_pos = jnp.sum(onehot * (jnp.cumsum(onehot, axis=0) - 1), axis=1)
    flat_index = flat_ids * capacity + slot_pos
    return (feat_float, inv_scale, normed, gate_value, flat_index)


def fill_slots(row_block, flat_index, experts, capacity, group_size):
    model_width = row_block.shape[1]
    buffer = (
        jnp.zeros((experts * capacity, model_width), row_block.dtype).at[flat_index].set(row_block)
    )
    return jnp.repeat(buffer.reshape(experts, capacity, model_width), group_size, axis=0)


def expert_rows(received, up_slice, down_slice):
    row_block = received.reshape(-1, received.shape[2])
    hidden = jnp.dot(row_block, up_slice, preferred_element_type=jnp.float32)
    sigma_vals = jax.nn.sigmoid(hidden)
    activated = (hidden * sigma_vals).astype(jnp.bfloat16)
    partial_value = jnp.dot(activated, down_slice, preferred_element_type=jnp.float32).astype(
        jnp.bfloat16
    )
    return (row_block, hidden, sigma_vals, activated, partial_value)


def expert_back(received, received_cot, up_slice, down_slice):
    row_block, hidden, sigma_vals, activated, partial_value = expert_rows(
        received, up_slice, down_slice
    )
    cot_block = received_cot.reshape(-1, received_cot.shape[2])
    gate_terms = jnp.sum(cot_block.astype(jnp.float32) * partial_value.astype(jnp.float32), axis=1)
    gate_terms = gate_terms.astype(jnp.bfloat16).reshape(received.shape[0], received.shape[1])
    act_grad = lax.dot_general(
        cot_block, down_slice, (((1,), (1,)), ((), ())), preferred_element_type=jnp.float32
    )
    hid_grad = (act_grad * sigma_vals * (1.0 + hidden * (1.0 - sigma_vals))).astype(jnp.bfloat16)
    grad_down = lax.dot_general(
        activated, cot_block, (((0,), (0,)), ((), ())), preferred_element_type=jnp.float32
    ).astype(jnp.bfloat16)
    grad_up = lax.dot_general(
        row_block, hid_grad, (((0,), (0,)), ((), ())), preferred_element_type=jnp.float32
    ).astype(jnp.bfloat16)
    input_part = lax.dot_general(
        hid_grad, up_slice, (((1,), (1,)), ((), ())), preferred_element_type=jnp.float32
    )
    input_part = input_part.astype(jnp.bfloat16).reshape(received.shape)
    return (input_part, gate_terms, grad_up, grad_down)


def group_total(returned, experts, group_size):
    shape_in = returned.shape
    summed = returned.reshape((experts, group_size) + shape_in[1:]).astype(jnp.float32).sum(axis=1)
    return summed.reshape((experts * shape_in[1],) + shape_in[2:])


def body(a_input, a_route, b_saved, b_grad, b_route, up_weight, down_weight, router):
    n_expert = lax.axis_size("expert")
    bit_count = lax.axis_size("pipe").bit_length() - 1
    experts = router.shape[2]
    group_size = n_expert // experts
    tokens = a_input.shape[1]
    top_count = a_route.shape[2]
    model_width = a_input.shape[2]
    capacity = tokens * top_count // experts + 2
    up_home = up_weight[0]
    down_home = down_weight[0]
    router_home = router[0]
    partner_pack = (b_saved[0], b_grad[0], b_route[0].astype(jnp.bfloat16))
    for bit_number in range(bit_count):
        partner_pack = partner(
            (partner_pack[0], partner_pack[1], partner_pack[2]), "pipe", bit_number
        )
    up_other, down_other, router_other = (up_home, down_home, router_home)
    b_features, b_cot, b_ids = partner_pack
    b_ids = b_ids.astype(jnp.int32)
    a_float, a_scale, a_normed, a_gate, a_index = route_plan(
        a_input[0], a_route[0], router_home, capacity
    )
    a_send = fill_slots(
        jnp.repeat(a_normed, top_count, axis=0), a_index, experts, capacity, group_size
    )
    b_float, b_scale, b_normed, b_gate, b_index = route_plan(
        b_features, b_ids, router_other, capacity
    )
    cot_rows = (
        (b_gate[:, :, None] * b_cot.astype(jnp.float32)[:, None, :])
        .astype(jnp.bfloat16)
        .reshape(-1, model_width)
    )
    b_send = fill_slots(
        jnp.repeat(b_normed, top_count, axis=0), b_index, experts, capacity, group_size
    )
    cot_send = fill_slots(cot_rows, b_index, experts, capacity, group_size)
    a_recv = lax.all_to_all(a_send, "expert", split_axis=0, concat_axis=0, tiled=True)
    a_part = expert_rows(a_recv, up_home, down_home)[4].reshape(a_recv.shape)
    a_back = lax.all_to_all(a_part, "expert", split_axis=0, concat_axis=0, tiled=True)
    b_recv, cot_recv = (
        lax.all_to_all(b_send, "expert", split_axis=0, concat_axis=0, tiled=True),
        lax.all_to_all(cot_send, "expert", split_axis=0, concat_axis=0, tiled=True),
    )
    input_part, gate_terms, up_grad, down_grad = expert_back(b_recv, cot_recv, up_other, down_other)
    back_input, back_terms = (
        lax.all_to_all(input_part, "expert", split_axis=0, concat_axis=0, tiled=True),
        lax.all_to_all(gate_terms, "expert", split_axis=0, concat_axis=0, tiled=True),
    )
    a_total = rounded(group_total(a_back, experts, group_size))
    input_total = rounded(group_total(back_input, experts, group_size))
    term_total = rounded(group_total(back_terms, experts, group_size))
    a_tok = a_total[a_index].reshape(tokens, top_count, model_width)
    a_out = (a_float + jnp.sum(a_gate[:, :, None] * a_tok, axis=1)).astype(jnp.bfloat16)
    input_tok = jnp.sum(input_total[b_index].reshape(tokens, top_count, model_width), axis=1)
    score_grad = term_total[b_index].reshape(tokens, top_count) * (1.0 - b_gate)
    onehot_b = (b_ids[:, :, None] == jnp.arange(experts, dtype=jnp.int32)).astype(jnp.float32)
    full_grad = jnp.sum(onehot_b * score_grad[:, :, None], axis=1)
    normed_grad = input_tok + jnp.dot(
        full_grad, router_other.astype(jnp.float32).T, precision=lax.Precision.HIGHEST
    )
    cubed = b_scale * b_scale * b_scale
    feature_grad = (
        b_scale * normed_grad
        - b_float * cubed * jnp.sum(normed_grad * b_float, axis=-1, keepdims=True) / model_width
    )
    b_out = (b_cot.astype(jnp.float32) + feature_grad).astype(jnp.bfloat16)
    for bit_number in range(bit_count):
        b_out = partner(b_out, "pipe", bit_number)
    a_next, b_next = from_behind((a_out, b_out), "pipe", 1)
    return (a_next[None], b_next[None], up_grad[None], down_grad[None])


def solution(mesh):
    return jax.shard_map(
        body,
        mesh=mesh,
        in_specs=(
            P("pipe", "expert", None),
            P("pipe", "expert", None),
            P("pipe", "expert", None),
            P("pipe", "expert", None),
            P("pipe", "expert", None),
            P("pipe", None, "expert"),
            P("pipe", "expert", None),
            P("pipe", None, None),
        ),
        out_specs=(
            P("pipe", "expert", None),
            P("pipe", "expert", None),
            P("pipe", None, "expert"),
            P("pipe", "expert", None),
        ),
        check_vma=False,
    )
```

profile of v0, /device:TPU:92, one launch (start us, length us, event | category | flops | bytes accessed | tf_op | source)
XLA Modules:
  0.0 967.4 jit_solution(11153496478981129024)
XLA Ops:
  0.7 2.7 collective-permute-done.4
  3.4 1.9 collective-permute-start.5
  5.3 20.8 %collective-permute-done.5 = bf16[128,3584]{1,0:T(8,128)(2,1)} collective-permute-done((bf16[128,3584]{1,0:T(8,128)(2,1)S(1)}, bf16[128,3584]{1,0:T(8,128)(2,1)}, u32[]{:S(2)}, u32[]{:S(2)}) %collective-permute-start.5) | collective-permute-done | bytes 917536 | tf_op jit(solution)/shard_map/ppermute | solution.py:16
  26.8 1.2 collective-permute-done.7
  27.9 1.7 collective-permute-start.8
  29.7 18.2 %collective-permute-done.8 = bf16[128,1]{0,1:T(2,128)(2,1)S(1)} collective-permute-done((bf16[128,1]{0,1:T(2,128)(2,1)S(1)}, bf16[128,1]{0,1:T(2,128)(2,1)S(1)}, u32[]{:S(2)}, u32[]{:S(2)}) %collective-permute-start.8) | collective-permute-done | bytes 288 | tf_op jit(solution)/shard_map/ppermute | solution.py:16
  48.6 17.0 %collective-permute-done.9 = bf16[128,1]{0,1:T(2,128)(2,1)S(1)} collective-permute-done((bf16[128,1]{0,1:T(2,128)(2,1)S(1)}, bf16[128,1]{0,1:T(2,128)(2,1)S(1)}, u32[]{:S(2)}, u32[]{:S(2)}) %collective-permute-start.9) | collective-permute-done | bytes 288 | tf_op jit(solution)/shard_map/ppermute | solution.py:16
  66.3 2.9 scatter_custom_fusion.2
  69.3 2.3 reshape.277
  71.6 4.2 broadcast_in_dim.20
  75.8 13.1 %all-to-all-start.3 = ((bf16[32,18,3584]{2,1,0:T(8,128)(2,1)}), bf16[32,18,3584]{2,1,0:T(8,128)(2,1)}, u32[]{:S(2)}, u32[]{:S(2)}) async-start(bf16[32,18,3584]{2,1,0:T(8,128)(2,1)} %bitcast.134), calls=%async_computation.3 | async-start | bytes 11010048 | tf_op jit(solution)/shard_map/all_to_all | solution.py:134
  89.0 2.8 collective-permute-done.1
  91.8 2.9 collective-permute-start.2
  95.2 140.0 %collective-permute-done.2 = bf16[128,3584]{1,0:T(8,128)(2,1)} collective-permute-done((bf16[128,3584]{1,0:T(8,128)(2,1)}, bf16[128,3584]{1,0:T(8,128)(2,1)}, u32[]{:S(2)}, u32[]{:S(2)}) %collective-permute-start.2) | collective-permute-done | bytes 917536 | tf_op jit(solution)/shard_map/ppermute | solution.py:16
  235.2 8.3 collective-permute-start.3
  243.9 1.0 gather_fusion.4
  244.9 35.7 %collective-permute-done.3 = bf16[128,3584]{1,0:T(8,128)(2,1)} collective-permute-done((bf16[128,3584]{1,0:T(8,128)(2,1)}, bf16[128,3584]{1,0:T(8,128)(2,1)}, u32[]{:S(2)}, u32[]{:S(2)}) %collective-permute-start.3) | collective-permute-done | bytes 917536 | tf_op jit(solution)/shard_map/ppermute | solution.py:16
  280.6 3.6 scatter_custom_fusion.1
  284.2 2.3 reshape.274
  286.5 4.2 broadcast_in_dim.19
  290.7 9.9 %all-to-all-start.2 = ((bf16[32,18,3584]{2,1,0:T(8,128)(2,1)}), bf16[32,18,3584]{2,1,0:T(8,128)(2,1)}, u32[]{:S(2)}, u32[]{:S(2)}) async-start(bf16[32,18,3584]{2,1,0:T(8,128)(2,1)} %bitcast.136), calls=%async_computation.2 | async-start | bytes 11010048 | tf_op jit(solution)/shard_map/all_to_all | solution.py:135
  300.6 1.4 fusion.7
  302.0 3.6 scatter_custom_fusion
  305.6 2.3 reshape.270
  307.9 118.3 %all-to-all-done.2 = bf16[32,18,3584]{2,1,0:T(8,128)(2,1)} async-done(((bf16[32,18,3584]{2,1,0:T(8,128)(2,1)}), bf16[32,18,3584]{2,1,0:T(8,128)(2,1)}, u32[]{:S(2)}, u32[]{:S(2)}) %all-to-all-start.2) | async-done | bytes 4128800 | tf_op jit(solution)/shard_map/all_to_all | solution.py:135
  426.1 4.1 broadcast_in_dim.17
  430.3 14.9 %all-to-all-start = ((bf16[32,18,3584]{2,1,0:T(8,128)(2,1)}), bf16[32,18,3584]{2,1,0:T(8,128)(2,1)}, u32[]{:S(2)}, u32[]{:S(2)}) async-start(bf16[32,18,3584]{2,1,0:T(8,128)(2,1)} %bitcast.135), calls=%async_computation | async-start | bytes 11010048 | tf_op jit(solution)/shard_map/all_to_all | solution.py:130
  445.2 7.4 reshape.279
  452.6 7.4 reshape.276
  460.0 3.5 fusion.22
  463.6 0.8 copy-done.9
  464.4 1.4 multiply_reduce_fusion
  466.5 4.1 fusion.32
  470.6 106.3 %all-to-all-done = bf16[32,18,3584]{2,1,0:T(8,128)(2,1)} async-done(((bf16[32,18,3584]{2,1,0:T(8,128)(2,1)}), bf16[32,18,3584]{2,1,0:T(8,128)(2,1)}, u32[]{:S(2)}, u32[]{:S(2)}) %all-to-all-start) | async-done | bytes 4128800 | tf_op jit(solution)/shard_map/all_to_all | solution.py:130
  576.9 9.9 %all-to-all-start.5 = ((bf16[32,1,18]{2,1,0:T(2,128)(2,1)}), bf16[32,1,18]{2,1,0:T(2,128)(2,1)S(1)}, u32[]{:S(2)}, u32[]{:S(2)}) async-start(bf16[32,1,18]{2,1,0:T(2,128)(2,1)} %convert_element_type.199), calls=%async_computation.5 | async-start | bytes 32768 | tf_op jit(solution)/shard_map/all_to_all | solution.py:140
  586.8 3.2 convolution_convert_fusion.1
  590.0 7.2 reshape.280
  597.2 12.2 %all-to-all-start.4 = ((bf16[32,18,3584]{2,1,0:T(8,128)(2,1)}), bf16[32,18,3584]{2,1,0:T(8,128)(2,1)}, u32[]{:S(2)}, u32[]{:S(2)}) async-start(bf16[32,18,3584]{2,1,0:T(8,128)(2,1)} %reshape.280), calls=%async_computation.4 | async-start | bytes 11010048 | tf_op jit(solution)/shard_map/all_to_all | solution.py:139
  609.4 7.3 reshape.272
  616.8 9.1 convolution_convert_fusion.2
  625.9 7.3 reshape.273
  633.1 109.3 %all-to-all-done.4 = bf16[32,18,3584]{2,1,0:T(8,128)(2,1)} async-done(((bf16[32,18,3584]{2,1,0:T(8,128)(2,1)}), bf16[32,18,3584]{2,1,0:T(8,128)(2,1)}, u32[]{:S(2)}, u32[]{:S(2)}) %all-to-all-start.4) | async-done | bytes 4128800 | tf_op jit(solution)/shard_map/all_to_all | solution.py:139
  742.4 8.4 all-to-all-start.1
  751.0 1.3 gather_fusion.2
  752.6 3.4 bitcast_reduce_fusion
  756.0 1.1 convert_element_type.182
  757.2 1.4 convert_element_type.183
  758.6 2.4 gather_fusion.1
  761.0 2.6 fusion.16
  763.6 1.9 fusion.6
  766.1 2.2 collective-permute-done.10
  768.3 42.7 %collective-permute-start.11 = (bf16[128,3584]{1,0:T(8,128)(2,1)}, bf16[128,3584]{1,0:T(8,128)(2,1)}, u32[]{:S(2)}, u32[]{:S(2)}) collective-permute-start(bf16[128,3584]{1,0:T(8,128)(2,1)} %collective-permute-done.10), channel_id=1, source_target_pairs={{0,64},{64,0},{32,96},{96,32},{128,192},{192,128},{160,224},{224,1... | collective-permute-start | bytes 2752520 | tf_op jit(solution)/shard_map/ppermute | solution.py:16
  811.0 1.0 gather_fusion.3
  812.0 76.1 %all-to-all-done.1 = bf16[32,18,3584]{2,1,0:T(8,128)(2,1)} async-done(((bf16[32,18,3584]{2,1,0:T(8,128)(2,1)}), bf16[32,18,3584]{2,1,0:T(8,128)(2,1)}, u32[]{:S(2)}, u32[]{:S(2)}) %all-to-all-start.1) | async-done | bytes 4128800 | tf_op jit(solution)/shard_map/all_to_all | solution.py:132
  888.1 3.4 bitcast_reduce_fusion.1
  892.1 2.4 gather_fusion
  894.5 7.9 collective-permute-start.12
  902.5 1.8 fusion.9
  904.3 47.7 %collective-permute-done.12 = bf16[128,3584]{1,0:T(8,128)(2,1)S(1)} collective-permute-done((bf16[128,3584]{1,0:T(8,128)(2,1)}, bf16[128,3584]{1,0:T(8,128)(2,1)S(1)}, u32[]{:S(2)}, u32[]{:S(2)}) %collective-permute-start.12) | collective-permute-done | bytes 917536 | tf_op jit(solution)/shard_map/ppermute | solution.py:16
  952.3 5.1 fusion.1
  957.4 2.9 fusion
  960.3 4.8 collective-permute-done.13
  965.1 0.9 copy.16
  966.0 0.9 copy.17
  (66 shorter events, 5.8 us)
Async XLA Ops:
  0.6 459.4 %copy-start = (bf16[1,3584,256]{2,1,0:T(8,128)(2,1)S(1)}, bf16[1,3584,256]{2,1,0:T(8,128)(2,1)}, u32[]{:S(2)}) copy-start(bf16[1,3584,256]{2,1,0:T(8,128)(2,1)} %param.15) | copy-start | bytes 5505028
  0.6 2.8 collective-permute-start.4
  3.4 22.7 %collective-permute-start.5 = (bf16[128,3584]{1,0:T(8,128)(2,1)S(1)}, bf16[128,3584]{1,0:T(8,128)(2,1)}, u32[]{:S(2)}, u32[]{:S(2)}) collective-permute-start(bf16[128,3584]{1,0:T(8,128)(2,1)S(1)} %collective-permute-done.4), channel_id=1, source_target_pairs={{0,64},{64,0},{32,96},{96,32},{128,192},{192,128},{160,224},{224,1... | collective-permute-start | bytes 2752520 | tf_op jit(solution)/shard_map/ppermute | solution.py:16
  26.1 40.0 %collective-permute-start.6 = (bf16[128,3584]{1,0:T(8,128)(2,1)}, bf16[128,3584]{1,0:T(8,128)(2,1)S(1)}, u32[]{:S(2)}, u32[]{:S(2)}) collective-permute-start(bf16[128,3584]{1,0:T(8,128)(2,1)} %collective-permute-done.5), channel_id=1, source_target_pairs={{0,128},{128,0},{32,160},{160,32},{64,192},{192,64},{96,224},{224,... | collective-permute-start | bytes 2752520 | tf_op jit(solution)/shard_map/ppermute | solution.py:16
  26.8 1.2 collective-permute-start.7
  27.9 20.0 %collective-permute-start.8 = (bf16[128,1]{0,1:T(2,128)(2,1)S(1)}, bf16[128,1]{0,1:T(2,128)(2,1)S(1)}, u32[]{:S(2)}, u32[]{:S(2)}) collective-permute-start(bf16[128,1]{0,1:T(2,128)(2,1)S(1)} %collective-permute-done.7), channel_id=1, source_target_pairs={{0,64},{64,0},{32,96},{96,32},{128,192},{192,128},{160,224},{224,1... | collective-permute-start | bytes 776 | tf_op jit(solution)/shard_map/ppermute | solution.py:16
  47.9 17.7 %collective-permute-start.9 = (bf16[128,1]{0,1:T(2,128)(2,1)S(1)}, bf16[128,1]{0,1:T(2,128)(2,1)S(1)}, u32[]{:S(2)}, u32[]{:S(2)}) collective-permute-start(bf16[128,1]{0,1:T(2,128)(2,1)S(1)} %collective-permute-done.8), channel_id=1, source_target_pairs={{0,128},{128,0},{32,160},{160,32},{64,192},{192,64},{96,224},{224,... | collective-permute-start | bytes 776 | tf_op jit(solution)/shard_map/ppermute | solution.py:16
  75.8 19.0 %copy-start.7 = (s32[1,128,1]{1,2,0:T(1,128)S(1)}, s32[1,128,1]{1,2,0:T(1,128)}, u32[]{:S(2)}) copy-start(s32[1,128,1]{1,2,0:T(1,128)} %param.11) | copy-start | bytes 1540
  75.8 167.7 %copy-start.6 = (bf16[1,3584,8]{1,2,0:T(8,128)(2,1)S(1)}, bf16[1,3584,8]{1,2,0:T(8,128)(2,1)}, u32[]{:S(2)}) copy-start(bf16[1,3584,8]{1,2,0:T(8,128)(2,1)} %param.17) | copy-start | bytes 172036
  75.8 210.7 %all-to-all-start.3 = ((bf16[32,18,3584]{2,1,0:T(8,128)(2,1)}), bf16[32,18,3584]{2,1,0:T(8,128)(2,1)}, u32[]{:S(2)}, u32[]{:S(2)}) async-start(bf16[32,18,3584]{2,1,0:T(8,128)(2,1)} %bitcast.134), calls=%async_computation.3 | async-start | bytes 11010048 | tf_op jit(solution)/shard_map/all_to_all | solution.py:134
  88.9 2.9 collective-permute-start.1
  91.8 143.4 %collective-permute-start.2 = (bf16[128,3584]{1,0:T(8,128)(2,1)}, bf16[128,3584]{1,0:T(8,128)(2,1)}, u32[]{:S(2)}, u32[]{:S(2)}) collective-permute-start(bf16[128,3584]{1,0:T(8,128)(2,1)} %collective-permute-done.1), channel_id=1, source_target_pairs={{0,64},{64,0},{32,96},{96,32},{128,192},{192,128},{160,224},{224,1... | collective-permute-start | bytes 2752520 | tf_op jit(solution)/shard_map/ppermute | solution.py:16
  235.2 45.4 %collective-permute-start.3 = (bf16[128,3584]{1,0:T(8,128)(2,1)}, bf16[128,3584]{1,0:T(8,128)(2,1)}, u32[]{:S(2)}, u32[]{:S(2)}) collective-permute-start(bf16[128,3584]{1,0:T(8,128)(2,1)} %collective-permute-done.2), channel_id=1, source_target_pairs={{0,128},{128,0},{32,160},{160,32},{64,192},{192,64},{96,224},{224,... | collective-permute-start | bytes 2752520 | tf_op jit(solution)/shard_map/ppermute | solution.py:16
  290.7 135.5 %all-to-all-start.2 = ((bf16[32,18,3584]{2,1,0:T(8,128)(2,1)}), bf16[32,18,3584]{2,1,0:T(8,128)(2,1)}, u32[]{:S(2)}, u32[]{:S(2)}) async-start(bf16[32,18,3584]{2,1,0:T(8,128)(2,1)} %bitcast.136), calls=%async_computation.2 | async-start | bytes 11010048 | tf_op jit(solution)/shard_map/all_to_all | solution.py:135
  430.3 146.7 %all-to-all-start = ((bf16[32,18,3584]{2,1,0:T(8,128)(2,1)}), bf16[32,18,3584]{2,1,0:T(8,128)(2,1)}, u32[]{:S(2)}, u32[]{:S(2)}) async-start(bf16[32,18,3584]{2,1,0:T(8,128)(2,1)} %bitcast.135), calls=%async_computation | async-start | bytes 11010048 | tf_op jit(solution)/shard_map/all_to_all | solution.py:130
  460.0 4.4 copy-start.5
  460.0 4.4 copy-start.8
  463.5 0.8 copy-start.9
  576.9 20.3 %all-to-all-start.5 = ((bf16[32,1,18]{2,1,0:T(2,128)(2,1)}), bf16[32,1,18]{2,1,0:T(2,128)(2,1)S(1)}, u32[]{:S(2)}, u32[]{:S(2)}) async-start(bf16[32,1,18]{2,1,0:T(2,128)(2,1)} %convert_element_type.199), calls=%async_computation.5 | async-start | bytes 32768 | tf_op jit(solution)/shard_map/all_to_all | solution.py:140
  597.2 145.2 %all-to-all-start.4 = ((bf16[32,18,3584]{2,1,0:T(8,128)(2,1)}), bf16[32,18,3584]{2,1,0:T(8,128)(2,1)}, u32[]{:S(2)}, u32[]{:S(2)}) async-start(bf16[32,18,3584]{2,1,0:T(8,128)(2,1)} %reshape.280), calls=%async_computation.4 | async-start | bytes 11010048 | tf_op jit(solution)/shard_map/all_to_all | solution.py:139
  742.4 145.7 %all-to-all-start.1 = ((bf16[32,18,3584]{2,1,0:T(8,128)(2,1)}), bf16[32,18,3584]{2,1,0:T(8,128)(2,1)}, u32[]{:S(2)}, u32[]{:S(2)}) async-start(bf16[32,18,3584]{2,1,0:T(8,128)(2,1)} %reshape.273), calls=%async_computation.1 | async-start | bytes 11010048 | tf_op jit(solution)/shard_map/all_to_all | solution.py:132
  763.6 2.1 copy-start.2
  765.6 2.7 collective-permute-start.10
  768.3 126.3 %collective-permute-start.11 = (bf16[128,3584]{1,0:T(8,128)(2,1)}, bf16[128,3584]{1,0:T(8,128)(2,1)}, u32[]{:S(2)}, u32[]{:S(2)}) collective-permute-start(bf16[128,3584]{1,0:T(8,128)(2,1)} %collective-permute-done.10), channel_id=1, source_target_pairs={{0,64},{64,0},{32,96},{96,32},{128,192},{192,128},{160,224},{224,1... | collective-permute-start | bytes 2752520 | tf_op jit(solution)/shard_map/ppermute | solution.py:16
  892.1 10.4 %copy-start.3 = (bf16[1,128,3584]{2,1,0:T(8,128)(2,1)S(1)}, bf16[1,128,3584]{2,1,0:T(8,128)(2,1)}, u32[]{:S(2)}) copy-start(bf16[1,128,3584]{2,1,0:T(8,128)(2,1)} %param.10) | copy-start | bytes 2752516
  894.5 57.8 %copy-start.10 = (f32[576,256]{1,0:T(8,128)S(1)}, f32[576,256]{1,0:T(8,128)}, u32[]{:S(2)}) copy-start(f32[576,256]{1,0:T(8,128)} %copy-done.9) | copy-start | bytes 1769476
  894.5 57.5 %collective-permute-start.12 = (bf16[128,3584]{1,0:T(8,128)(2,1)}, bf16[128,3584]{1,0:T(8,128)(2,1)S(1)}, u32[]{:S(2)}, u32[]{:S(2)}) collective-permute-start(bf16[128,3584]{1,0:T(8,128)(2,1)} %collective-permute-done.11), channel_id=1, source_target_pairs={{0,128},{128,0},{32,160},{160,32},{64,192},{192,64},{96,224},{224,... | collective-permute-start | bytes 2752520 | tf_op jit(solution)/shard_map/ppermute | solution.py:16
  904.2 53.1 %copy-start.4 = (bf16[576,3584]{1,0:T(8,128)(2,1)S(1)}, bf16[576,3584]{1,0:T(8,128)(2,1)}, u32[]{:S(2)}) copy-start(bf16[576,3584]{1,0:T(8,128)(2,1)} %reshape.279) | copy-start | bytes 12386308
  904.2 56.0 %collective-permute-start = (bf16[128,3584]{1,0:T(8,128)(2,1)S(1)}, bf16[128,3584]{1,0:T(8,128)(2,1)S(1)}, u32[]{:S(2)}, u32[]{:S(2)}) collective-permute-start(bf16[128,3584]{1,0:T(8,128)(2,1)S(1)} %fusion.9), channel_id=1, source_target_pairs={{0,32},{32,64},{64,96},{96,128},{128,160},{160,192},{192,224},{224... | collective-permute-start | bytes 2752520 | tf_op jit(solution)/shard_map/ppermute | solution.py:21
  952.1 13.0 %collective-permute-start.13 = (bf16[128,3584]{1,0:T(8,128)(2,1)S(1)}, bf16[128,3584]{1,0:T(8,128)(2,1)S(1)}, u32[]{:S(2)}, u32[]{:S(2)}) collective-permute-start(bf16[128,3584]{1,0:T(8,128)(2,1)S(1)} %collective-permute-done.12), channel_id=1, source_target_pairs={{0,32},{32,64},{64,96},{96,128},{128,160},{160,192},{192,224},{224... | collective-permute-start | bytes 2752520 | tf_op jit(solution)/shard_map/ppermute | solution.py:21
  965.1 1.9 copy-start.1
where the time goes:
time: 986 us; the launch traced here: 967 us
  waiting for transfers between devices  703 us (71%)
  starting transfers between devices  135 us (14%)
  local copies, waits for them, and re-layouts  69 us (7%)
  matrix products  32.7 us (3%)
  other arithmetic  26 us (3%)
    ppermute x12, waiting for transfers between devices, partner(): return lax.ppermute(block, axis, route)  288 us
    all_to_all x1, waiting for transfers between devices, body(): lax.all_to_all(cot_send, 'expert', split_axis=0, concat_axis=0, tiled=True)  118 us
    all_to_all x1, waiting for transfers between devices, body(): lax.all_to_all(input_part, 'expert', split_axis=0, concat_axis=0, tiled=T...  109 us
    all_to_all x1, waiting for transfers between devices, body(): lax.all_to_all(a_send, 'expert', split_axis=0, concat_axis=0, tiled=True)  106 us
    all_to_all x1, waiting for transfers between devices, body(): lax.all_to_all(a_part, 'expert', split_axis=0, concat_axis=0, tiled=True)  76.1 us
    ppermute x12, starting transfers between devices, partner(): return lax.ppermute(block, axis, route)  66.5 us
  transfers between devices with their start and end apart: 20, of which 15 were waited for; matrix products, arithmetic and copies ran while one was open for 11% of the time, Pallas kernels for 0%

commit v1 on v0

v1 whole, which is shorter than its diff:
```python
import jax
import jax.numpy as jnp
from jax import lax
from jax.experimental import pallas as pl
from jax.experimental.pallas import tpu as pltpu
from jax.sharding import PartitionSpec as P

EPS = 1e-06
MESH = pl.DeviceIdType.MESH
TOK = 128
D = 3584
CAP = 18
EXPERTS = 8
SIDE = 4
PLANE = 16
PARTS = 4
W = D // PARTS
WIDE = 9 * W
BF = jnp.bfloat16
NEAR = sorted(
    [(i, j) for i in range(SIDE) for j in range(SIDE) if i or j],
    key=lambda s: min(s[0], SIDE - s[0]) + min(s[1], SIDE - s[1]),
)


class Place:
    def __init__(self):
        self.pipe = lax.axis_index("pipe")
        self.expert = lax.axis_index("expert")
        self.half = lax.rem(self.expert, 2)
        self.spot = self.expert // 2
        self.x = self.spot // SIDE
        self.y = lax.rem(self.spot, SIDE)
        self.across = self.expert + 1 - 2 * self.half

    def spot_at(self, dx, dy):
        return lax.rem(self.x + dx, SIDE) * SIDE + lax.rem(self.y + dy, SIDE)

    def plane(self, spot):
        return (self.pipe, spot * 2 + self.half)


def remote(src, dst, send, recv, device):
    return pltpu.make_async_remote_copy(
        src_ref=src, dst_ref=dst, send_sem=send, recv_sem=recv, device_id=device, device_id_type=MESH
    )


def cols(at, width=W):
    return pl.ds(pl.multiple_of(at * W, 128), width)


def rows16(e):
    return pl.ds(pl.multiple_of(e * 16, 16), 16)


def selector(kind, code, part=0):
    row = lax.broadcasted_iota(jnp.int32, (TOK, TOK), 0)
    e, slot = code // 32, code % 32
    if kind == "own0":
        to, ok = slot, slot < 16
    elif kind == "own1":
        to, ok = slot - 16, slot >= 16
    elif kind == "far1":
        to, ok = slot + 2, slot < 14
    else:
        to, ok = slot - 14 + 4 * part, slot >= 14
    return ((row == e * 16 + to) & ok).astype(jnp.float32).astype(BF)


def fill_selectors(sel, t, own_code, far_code):
    sel[t, 0] = selector("own0", own_code)
    sel[t, 1] = selector("own1", own_code)
    sel[t, 2] = selector("far1", far_code)
    for q in range(PARTS):
        sel[t, 3 + q] = selector("left", far_code, q)


def dot(a, b):
    return jnp.dot(a, b, preferred_element_type=jnp.float32)


def dispatch_kernel(
    ax, bx, bc, acode, bcode, ra, rbx, rbc, bc_own, far_codes,
    own_a, far_a, got_b, codes, send_a, send_bx, send_bc, left, sel,
    zsend, zrecv, csend, crecv, psend, precv, local,
):
    me = Place()
    across = (me.pipe, me.across)
    mirror = (7 - me.pipe, me.expert)
    mirror_across = (7 - me.pipe, me.across)
    barrier = pltpu.get_barrier_semaphore()
    greet = [me.plane(me.spot_at(i, j)) for i, j in NEAR] + [across, mirror, mirror_across]
    for device in greet:
        pl.semaphore_signal(barrier, inc=1, device_id=device, device_id_type=MESH)
    load = pltpu.make_async_copy(ax, own_a, local.at[0])
    load.start()
    pl.semaphore_wait(barrier, len(greet))

    small = [
        remote(acode, codes.at[0], csend.at[0], crecv.at[0], across),
        remote(bcode, codes.at[1], csend.at[1], crecv.at[1], mirror),
        remote(bcode, codes.at[2], csend.at[2], crecv.at[2], mirror_across),
    ]
    for copy in small:
        copy.start()

    def z_copy(lane, q):
        src, dst, to = [
            (ax, far_a, across),
            (bx, got_b.at[0], mirror),
            (bx, got_b.at[1], mirror_across),
            (bc, got_b.at[2], mirror),
            (bc, got_b.at[3], mirror_across),
        ][lane]
        return remote(src.at[:, cols(q)], dst.at[:, cols(q)], zsend.at[lane, q], zrecv.at[lane, q], to)

    for lanes in ((0,), (1, 2), (3, 4)):
        @pl.loop(0, PARTS)
        def _(q):
            for lane in lanes:
                z_copy(lane, q).start()

    def spread(t, send, recv, at):
        pltpu.make_async_copy(
            send.at[rows16(me.spot // 2), cols(at)], recv.at[me.spot, :, cols(at)], precv.at[t]
        ).start()
        for i, j in NEAR:
            to = me.spot_at(i, j)
            remote(
                send.at[rows16(to // 2), cols(at)], recv.at[me.spot, :, cols(at)],
                psend.at[t], precv.at[t], me.plane(to),
            ).start()

    load.wait()
    sel[0, 0] = selector("own0", acode[0:1, :])

    @pl.loop(0, PARTS)
    def _(q):
        send_a[:, cols(q)] = dot(sel[0, 0], own_a[:, cols(q)]).astype(BF)
        spread(0, send_a, ra, q)

    small[0].wait()
    fill_selectors(sel, 0, acode[0:1, :], codes[0, 0:1, :])
    left[...] = jnp.zeros_like(left)

    @pl.loop(0, PARTS)
    def _(q):
        z_copy(0, q).wait()
        far = far_a[:, cols(q)]
        send_a[:, cols(PARTS + q)] = (dot(sel[0, 1], own_a[:, cols(q)]) + dot(sel[0, 2], far)).astype(BF)
        left[...] += dot(sel[0, 3 + q], far)
        spread(0, send_a, ra, PARTS + q)

    send_a[:, 2 * D:] = left[...].astype(BF)
    spread(0, send_a, ra, 2 * PARTS)

    small[1].wait()
    small[2].wait()
    fill_selectors(sel, 1, codes[1, 0:1, :], codes[2, 0:1, :])
    for t, send, recv in ((1, send_bx, rbx), (2, send_bc, rbc)):
        near_at, far_at = 2 * t - 2, 2 * t - 1
        left[...] = jnp.zeros_like(left)

        @pl.loop(0, PARTS)
        def _(q):
            z_copy(2 * t - 1, q).wait()
            own = got_b[near_at, :, cols(q)]
            send[:, cols(q)] = dot(sel[1, 0], own).astype(BF)
            spread(t, send, recv, q)
            z_copy(2 * t, q).wait()
            far = got_b[far_at, :, cols(q)]
            send[:, cols(PARTS + q)] = (dot(sel[1, 1], own) + dot(sel[1, 2], far)).astype(BF)
            left[...] += dot(sel[1, 3 + q], far)
            spread(t, send, recv, PARTS + q)

        send[:, 2 * D:] = left[...].astype(BF)
        spread(t, send, recv, 2 * PARTS)

    out_c = pltpu.make_async_copy(got_b.at[2], bc_own, local.at[1])
    out_c.start()
    out_codes = pltpu.make_async_copy(codes, far_codes, local.at[2])
    out_codes.start()
    for t, recv in ((0, ra), (1, rbx), (2, rbc)):
        most = recv.at[pl.ds(0, PLANE - 1)]
        remote(most, most, psend.at[t], precv.at[t], across).wait_send()
        pltpu.make_async_copy(recv, recv, precv.at[t]).wait()
    out_c.wait()
    out_codes.wait()


def dispatch(ax, bx, bc, acode, bcode):
    block = jax.ShapeDtypeStruct((PLANE, 16, WIDE), BF)
    anywhere = pl.BlockSpec(memory_space=pl.ANY)
    inside = pl.BlockSpec(memory_space=pltpu.VMEM)
    dma = pltpu.SemaphoreType.DMA
    return pl.pallas_call(
        dispatch_kernel,
        name="dispatch",
        out_shape=(block, block, block, jax.ShapeDtypeStruct((TOK, D), BF),
                   jax.ShapeDtypeStruct((3, 8, TOK), jnp.int32)),
        in_specs=[anywhere] * 3 + [inside] * 2,
        out_specs=(anywhere,) * 5,
        scratch_shapes=[
            pltpu.VMEM((TOK, D), BF), pltpu.VMEM((TOK, D), BF), pltpu.VMEM((4, TOK, D), BF),
            pltpu.VMEM((3, 8, TOK), jnp.int32),
            pltpu.VMEM((TOK, WIDE), BF), pltpu.VMEM((TOK, WIDE), BF), pltpu.VMEM((TOK, WIDE), BF),
            pltpu.VMEM((TOK, W), jnp.float32), pltpu.VMEM((2, 3 + PARTS, TOK, TOK), BF),
            dma((5, PARTS)), dma((5, PARTS)), dma((3,)), dma((3,)), dma((3,)), dma((3,)), dma((3,)),
        ],
        compiler_params=pltpu.CompilerParams(collective_id=1, has_side_effects=True, vmem_limit_bytes=40 << 20),
    )(ax, bx, bc, acode, bcode)


def collect_kernel(
    sa, sb, xa, cb, ua, ub, oa, ob,
    ga, gb, base, own, far, psend, precv, zsend, zrecv, local,
):
    me = Place()
    a_to = lax.rem(me.pipe + 1, 8)
    a_from = lax.rem(me.pipe + 7, 8)
    b_to = lax.rem(8 - me.pipe, 8)
    stays = b_to == me.pipe
    barrier = pltpu.get_barrier_semaphore()
    greet = [me.plane(me.spot_at(i, j)) for i, j in NEAR]
    greet += [(a_to, me.expert), (a_to, me.across), (a_from, me.expert), (a_from, me.across), (b_to, me.across)]
    for device in greet:
        pl.semaphore_signal(barrier, inc=1, device_id=device, device_id_type=MESH)

    @pl.when(jnp.logical_not(stays))
    def _():
        pl.semaphore_signal(barrier, inc=1, device_id=(b_to, me.expert), device_id_type=MESH)

    loads = [
        pltpu.make_async_copy(xa, base.at[0], local.at[0]),
        pltpu.make_async_copy(cb, base.at[1], local.at[1]),
    ]
    for copy in loads:
        copy.start()
    pl.semaphore_wait(barrier, len(greet) + 1 - stays.astype(jnp.int32))

    def spread(t, send, recv, at, sem):
        pltpu.make_async_copy(
            send.at[me.spot, :, cols(at)], recv.at[me.spot, :, cols(at)], precv.at[t, sem]
        ).start()
        for i, j in NEAR:
            to = me.spot_at(i, j)
            remote(
                send.at[to, :, cols(at)], recv.at[me.spot, :, cols(at)],
                psend.at[t], precv.at[t, sem], me.plane(to),
            ).start()

    tensors = ((0, sa, ga, ua, oa, a_to), (1, sb, gb, ub, ob, b_to))
    for t, send, recv, u, out, to in tensors:
        spread(t, send, recv, 2 * PARTS, PARTS)

        @pl.loop(0, PARTS)
        def _(q):
            spread(t, send, recv, PARTS + q, q)
            spread(t, send, recv, q, q)

    for copy in loads:
        copy.wait()

    def flat(ref, at):
        return ref[:, :, cols(at)].reshape(PLANE * 16, W)

    for t, send, recv, u, out, to in tensors:
        edge = recv.at[:, :, pl.ds(2 * D, W)]
        pltpu.make_async_copy(edge, edge, precv.at[t, PARTS]).wait()

        @pl.loop(0, PARTS)
        def _(q):
            both = recv.at[:, :, pl.ds(0, 2 * W)]
            pltpu.make_async_copy(both, both, precv.at[t, q]).wait()
            second = flat(recv, PARTS + q)
            far[t, :, cols(q)] = (dot(u[2], second) + dot(u[3 + q], flat(recv, 2 * PARTS))).astype(BF)
            remote(
                far.at[t, :, cols(q)], out.at[1, :, cols(q)],
                zsend.at[t, 1, q], zrecv.at[t, 1, q], (to, me.across),
            ).start()
            own[t, :, cols(q)] = (
                base[t, :, cols(q)].astype(jnp.float32) + dot(u[0], flat(recv, q)) + dot(u[1], second)
            ).astype(BF)
            send_own = remote(
                own.at[t, :, cols(q)], out.at[0, :, cols(q)],
                zsend.at[t, 0, q], zrecv.at[t, 0, q], (to, me.expert),
            )
            if t == 0:
                send_own.start()
            else:
                @pl.when(stays)
                def _():
                    pltpu.make_async_copy(
                        own.at[t, :, cols(q)], out.at[0, :, cols(q)], zrecv.at[t, 0, q]
                    ).start()

                @pl.when(jnp.logical_not(stays))
                def _():
                    send_own.start()

    for t, send, recv, u, out, to in tensors:
        most = recv.at[pl.ds(0, PLANE - 1)]
        remote(most, most, psend.at[t], precv.at[t, 0], (to, me.across)).wait_send()

        @pl.loop(0, PARTS)
        def _(q):
            remote(
                far.at[t, :, cols(q)], out.at[1, :, cols(q)],
                zsend.at[t, 1, q], zrecv.at[t, 1, q], (to, me.across),
            ).wait()
            if t == 0:
                remote(
                    own.at[t, :, cols(q)], out.at[0, :, cols(q)],
                    zsend.at[t, 0, q], zrecv.at[t, 0, q], (to, me.expert),
                ).wait()
            else:
                @pl.when(jnp.logical_not(stays))
                def _():
                    remote(
                        own.at[t, :, cols(q)], out.at[0, :, cols(q)],
                        zsend.at[t, 0, q], zrecv.at[t, 0, q], (to, me.expert),
                    ).wait()

                @pl.when(stays)
                def _():
                    pltpu.make_async_copy(
                        own.at[t, :, cols(q)], out.at[0, :, cols(q)], zrecv.at[t, 0, q]
                    ).wait()


def collect(sa, sb, xa, cb, ua, ub):
    pair = jax.ShapeDtypeStruct((2, TOK, D), BF)
    anywhere = pl.BlockSpec(memory_space=pl.ANY)
    inside = pl.BlockSpec(memory_space=pltpu.VMEM)
    dma = pltpu.SemaphoreType.DMA
    return pl.pallas_call(
        collect_kernel,
        name="collect",
        out_shape=(pair, pair),
        in_specs=[anywhere] * 4 + [inside] * 2,
        out_specs=(anywhere,) * 2,
        scratch_shapes=[
            pltpu.VMEM((PLANE, 16, WIDE), BF), pltpu.VMEM((PLANE, 16, WIDE), BF),
            pltpu.VMEM((2, TOK, D), BF), pltpu.VMEM((2, TOK, D), BF), pltpu.VMEM((2, TOK, D), BF),
            dma((2,)), dma((2, PARTS + 1)), dma((2, 2, PARTS)), dma((2, 2, PARTS)), dma((2,)),
        ],
        compiler_params=pltpu.CompilerParams(collective_id=2, has_side_effects=True, vmem_limit_bytes=40 << 20),
    )(sa, sb, xa, cb, ua, ub)


def slot_code(route):
    ids = route.reshape(TOK)
    same = ids[:, None] == ids[None, :]
    earlier = jnp.arange(TOK)[:, None] < jnp.arange(TOK)[None, :]
    slot = jnp.sum((same & earlier).astype(jnp.int32), axis=0)
    return jnp.broadcast_to((ids * 32 + slot)[None, :], (8, TOK)).astype(jnp.int32)


def unslot(own_code, far_code):
    lane = jnp.arange(PLANE * 16, dtype=jnp.int32)[None, :]
    e_of, r_of = lane // 32, lane % 16

    def one(code, to, ok):
        return ((code // 32 == e_of) & (r_of == to) & ok).astype(BF)

    own, far = own_code[:, None], far_code[:, None]
    so, sf = own % 32, far % 32
    parts = [one(own, so, so < 16), one(own, so - 16, so >= 16), one(far, sf + 2, sf < 14)]
    parts += [one(far, sf - 14 + 4 * q, sf >= 14) for q in range(PARTS)]
    return jnp.stack(parts)


def to_rows(block):
    flat = block.reshape(PLANE * 16, WIDE)
    tail = flat[:, 2 * D:].reshape(PLANE, PARTS, 4, W).transpose(0, 2, 1, 3).reshape(PLANE * 4, D)
    return jnp.concatenate([flat[:, :D], flat[:, D:2 * D], tail], axis=0)


def from_rows(rows):
    n = PLANE * 16
    tail = rows[2 * n:].reshape(PLANE, 4, PARTS, W).transpose(0, 2, 1, 3).reshape(n, W)
    return jnp.concatenate([rows[:n], rows[n:2 * n], tail], axis=1).reshape(PLANE, 16, WIDE)


def plan(rows, column):
    x = rows.astype(jnp.float32)
    scale = lax.rsqrt(jnp.mean(x * x, axis=1, keepdims=True) + EPS)
    normed = (x * scale).astype(BF)
    score = jnp.sum(normed.astype(jnp.float32) * column[None, :], axis=1, keepdims=True)
    return x, scale, normed, jax.nn.sigmoid(score)


def mm(a, b, ca, cb):
    return lax.dot_general(a, b, (((ca,), (cb,)), ((), ())), preferred_element_type=jnp.float32)


def body(a_input, a_route, b_saved, b_grad, b_route, up_weight, down_weight, router):
    up, down = up_weight[0], down_weight[0]
    group = lax.axis_size("expert") // EXPERTS
    mine = lax.axis_index("expert") // group
    column = lax.dynamic_slice(router[0], (0, mine), (D, 1))[:, 0].astype(jnp.float32)
    a_code, b_code = slot_code(a_route[0]), slot_code(b_route[0])
    ra, rbx, rbc, c_own, codes = dispatch(a_input[0], b_saved[0], b_grad[0], a_code, b_code)
    ua = unslot(a_code[0], codes[0, 0])
    ub = unslot(codes[1, 0], codes[2, 0])

    _, _, normed, gate = plan(to_rows(ra), column)
    hidden = mm(normed, up, 1, 0)
    act = (hidden * jax.nn.sigmoid(hidden)).astype(BF)
    a_ret = from_rows((gate * mm(act, down, 1, 0)).astype(BF))

    x, scale, normed, gate = plan(to_rows(rbx), column)
    cot = (gate * to_rows(rbc).astype(jnp.float32)).astype(BF)
    hidden = mm(normed, up, 1, 0)
    sig = jax.nn.sigmoid(hidden)
    act = (hidden * sig).astype(BF)
    act_grad = mm(cot, down, 1, 1)
    gate_part = jnp.sum(act.astype(jnp.float32) * act_grad, axis=1, keepdims=True)
    hid_grad = (act_grad * sig * (1.0 + hidden * (1.0 - sig))).astype(BF)
    grad = mm(hid_grad, up, 1, 1) + (gate_part * (1.0 - gate)) * column[None, :]
    along = jnp.sum(grad * x, axis=1, keepdims=True)
    b_ret = from_rows((scale * grad - x * (scale * scale * scale) * along / D).astype(BF))

    out_a, out_b = collect(a_ret, b_ret, a_input[0], c_own, ua, ub)
    down_grad = mm(act, cot, 0, 0).astype(BF)
    up_grad = mm(normed, hid_grad, 0, 0).astype(BF)
    a_next = (out_a[0].astype(jnp.float32) + out_a[1].astype(jnp.float32)).astype(BF)
    b_next = (out_b[0].astype(jnp.float32) + out_b[1].astype(jnp.float32)).astype(BF)
    return a_next[None], b_next[None], up_grad[None], down_grad[None]


def solution(mesh):
    rows = P("pipe", "expert", None)
    return jax.shard_map(
        body,
        mesh=mesh,
        in_specs=(rows, rows, rows, rows, rows, P("pipe", None, "expert"), rows, P("pipe", None, None)),
        out_specs=(rows, rows, P("pipe", None, "expert"), rows),
        check_vma=False,
    )
```

time: 986 us -> 389 us (0.39); the launches traced: 967 us -> 389 us
  waiting for transfers between devices: 703 us -> 0 us
  Pallas kernels: 0 us -> 297 us
  starting transfers between devices: 135 us -> 0 us
  local copies, waits for them, and re-layouts: 69 us -> 35.8 us
    all_to_all x6 -> x0, waiting for transfers between devices: 410 us -> none  [the longest x1 118 us: body(): lax.all_to_all(cot_send, 'expert', split_axis=0, concat_axis=0, tiled=True)]
    pallas_call x0 -> x2, Pallas kernels: none -> 297 us  [the longest x1 186 us: dispatch(): pl.pallas_call(dispatch_kernel, name='dispatch', out_shape=(block, block,...]
    ppermute x14 -> x0, waiting for transfers between devices: 293 us -> none  [the longest x12 288 us: partner(): return lax.ppermute(block, axis, route)]
    all_to_all x6 -> x0, starting transfers between devices: 68.5 us -> none  [the longest x1 14.9 us: body(): lax.all_to_all(a_send, 'expert', split_axis=0, concat_axis=0, tiled=True)]
    ppermute x14 -> x0, starting transfers between devices: 66.8 us -> none  [the longest x12 66.5 us: partner(): return lax.ppermute(block, axis, route)]
    reshape x8 -> x9, local copies, waits for them, and re-layouts: 43.4 us -> 11.5 us  [the longest x5 7.36 us: to_rows(): flat[:, 2 * D:].reshape(PLANE, PARTS, 4, W).transpose(0, 2, 1, 3)]
    slice x0 -> x12, local copies, waits for them, and re-layouts: none -> 14.2 us  [the longest x3 6.4 us: to_rows(): return jnp.concatenate([flat[:, :D], flat[:, D:2 * D], tail], axis=0)]
    broadcast_in_dim x3 -> x2, local copies, waits for them, and re-layouts: 12.5 us -> 0.01 us  [slot_code(): jnp.broadcast_to((ids * 32 + slot)[None, :], (8, TOK)).astype(jnp.int32)]
  transfers between devices with their start and end apart: 20 -> 0, of which waited for: 15 -> 0; matrix products, arithmetic and copies ran while one was open for 11% -> 0% of each run, Pallas kernels for 0% -> 0%
where the time goes in v1:
time: 389 us
  Pallas kernels  297 us (76%)
  local copies, waits for them, and re-layouts  35.8 us (9%)
  other arithmetic  31.6 us (8%)
  matrix products  23.7 us (6%)
    pallas_call x1, Pallas kernels, dispatch(): pl.pallas_call(dispatch_kernel, name='dispatch', out_shape=(block, block,...  186 us
    pallas_call x1, Pallas kernels, collect(): pl.pallas_call(collect_kernel, name='collect', out_shape=(pair, pair), in...  110 us
    dot_general x6, matrix products, mm(): lax.dot_general(a, b, (((ca,), (cb,)), ((), ())), preferred_element_type=...  23.7 us
    convert_element_type x1, other arithmetic, body(): (scale * grad - x * (scale * scale * scale) * along / D).astype(BF)  8.9 us
    concatenate x2, other arithmetic, from_rows(): jnp.concatenate([rows[:n], rows[n:2 * n], tail], axis=1)  7.92 us

profile of v1, /device:TPU:92, one launch (start us, length us, event | category | flops | bytes accessed | tf_op | source)
XLA Modules:
  0.0 388.7 jit_solution(3206118041063391740)
XLA Ops:
  0.7 0.9 convert_reduce_fusion
  1.6 0.7 multiply_add_fusion.1
  2.2 0.8 convert_reduce_fusion.1
  3.1 0.7 broadcast_compare_fusion.6
  3.8 0.9 convert_reduce_fusion.2
  4.7 1.2 copy-done.4
  5.8 1.2 copy-done.6
  7.0 1.2 copy-done.7
  8.2 186.3 %dispatch.1 = (bf16[16,16,8064]{2,1,0:T(8,128)(2,1)S(1)}, bf16[16,16,8064]{2,1,0:T(8,128)(2,1)S(1)}, bf16[16,16,8064]{2,1,0:T(8,128)(2,1)}, bf16[128,3584]{1,0:T(8,128)(2,1)S(1)}, s32[3,8,128]{2,1,0:T(8,128)S(1)}) custom-call(bf16[128,3584]{1,0:T(8,128)(2,1)S(1)} %bitcast.99, bf16[128,3584]{1,0:T(8,128)(2,1)S(1)} %bitcast.101, ...), custom_call_target="tpu_custom_call" | custom-call | tf_op jit(solution)/shard_map/dispatch/pallas_call | solution.py:197
  194.7 0.1 fusion.30
  194.8 0.1 fusion.32
  194.9 0.1 fusion.44
  195.1 0.1 fusion.46
  195.2 0.1 fusion.48
  195.3 0.2 fusion.50
  195.5 0.2 fusion.52
  195.7 0.1 fusion.34
  195.9 0.1 fusion.36
  196.0 0.1 fusion.38
  196.1 0.1 fusion.40
  196.3 0.1 fusion.42
  196.4 0.1 stack.9.ua
  196.5 0.1 stack.11.ub
  196.6 2.2 fusion.64
  198.8 0.9 reshape.2238
  199.7 1.3 copy.19
  201.1 0.1 copy.23
  201.1 2.7 fusion.2
  203.8 1.4 multiply_reduce_fusion
  205.3 0.8 slice.91
  206.1 2.1 fusion.62
  208.1 1.9 reshape.2234
  210.0 1.3 copy.17
  211.4 0.8 copy-done.18
  212.2 2.5 fusion
  214.7 0.8 slice.100
  215.5 2.1 fusion.63
  217.7 1.9 reshape.2241
  219.6 1.2 copy.20
  220.9 3.5 fusion.16
  224.4 0.2 copy-done.22
  224.5 1.5 multiply_reduce_fusion.2
  226.0 3.0 fusion.10
  229.1 3.4 fusion.9
  232.5 3.1 fusion.8
  235.7 8.9 %fusion.7 = bf16[576,3584]{1,0:T(8,128)(2,1)} fusion(f32[576,3584]{1,0:T(8,128)S(1)} %get-tuple-element.68, f32[576]{0:T(1024)S(1)} %get-tuple-element.18, f32[576]{0:T(1024)S(1)} %get-tuple-element.50, f32[576]{0:T(1024)S(1)} %get-tuple-element.71, f32[576]{0:T(1024)S(1)} %get-tuple-element.51, f32[3584]{0:T(1024)S(1)} %convert_reduce_fusion.2, ...), kind=kLoop, calls=%fused_computation.13 | loop fusion | flops 28901376 | bytes 16538624 | tf_op jit(solution)/shard_map/convert_element_type | solution.py:423
  244.6 9.2 %multiply_convert_fusion.1 = bf16[576,3584]{1,0:T(8,128)(2,1)} fusion(f32[576]{0:T(1024)S(1)} %add_divide_fusion.2, bf16[1,256,3584]{2,1,0:T(8,128)(2,1)} %param.14, bf16[1,3584,256]{2,1,0:T(8,128)(2,1)S(1)} %copy-done, f32[576]{0:T(1024)S(1)} %get-tuple-element.72, bf16[64,3584]{1,0:T(8,128)(2,1)} %bitcast.116, bf16[256,3584]{1,0:T(8,128)(2,1)} %get-tuple-element.37, ...), kind=kOutput, calls=%fused_computation.18 | convolution fusion | flops 2135310336 | bytes 11932160 | tf_op jit(solution)/shard_map/dot_general | solution.py:395
  253.7 4.1 %fusion.61 = (bf16[256,3584]{1,0:T(8,128)(2,1)}, bf16[256,3584]{1,0:T(8,128)(2,1)}) fusion(bf16[576,3584]{1,0:T(8,128)(2,1)} %multiply_convert_fusion.1), kind=kLoop, calls=%fused_computation.153 | loop fusion | bytes 7340032 | tf_op jit(solution)/shard_map/slice | solution.py:383
  257.9 0.9 reshape.2236
  258.8 1.2 copy.28
  260.0 0.9 concatenate.32
  260.8 4.0 %pad_maximum_fusion.1.sa = bf16[16,16,8064]{2,1,0:T(8,128)(2,1)} fusion(bf16[16,16,896]{2,1,0:T(8,128)(2,1)} %concatenate.32, bf16[16,16,3584]{2,1,0:T(8,128)(2,1)} %bitcast.110, bf16[16,16,3584]{2,1,0:T(8,128)(2,1)} %bitcast.109), kind=kLoop, calls=%fused_computation.25 | loop fusion | flops 12386304 | bytes 8257536 | tf_op jit(solution)/shard_map/concatenate | solution.py:383
  264.8 1.0 copy-done.14
  265.8 2.0 fusion.60
  267.8 0.9 reshape.2243
  268.7 1.2 copy.27
  269.9 0.9 concatenate.38
  270.8 4.0 %pad_maximum_fusion.3.sb = bf16[16,16,8064]{2,1,0:T(8,128)(2,1)} fusion(bf16[16,16,896]{2,1,0:T(8,128)(2,1)} %concatenate.38, bf16[16,16,3584]{2,1,0:T(8,128)(2,1)} %bitcast.112, bf16[16,16,3584]{2,1,0:T(8,128)(2,1)} %bitcast.111), kind=kLoop, calls=%fused_computation.27 | loop fusion | flops 12386304 | bytes 8257536 | tf_op jit(solution)/shard_map/concatenate | solution.py:383
  274.7 1.0 copy-done.1
  275.7 0.3 copy-done.5
  276.0 0.3 copy-done.9
  276.2 110.2 %collect.1 = (bf16[2,128,3584]{2,1,0:T(8,128)(2,1)S(1)}, bf16[2,128,3584]{2,1,0:T(8,128)(2,1)S(1)}) custom-call(bf16[16,16,8064]{2,1,0:T(8,128)(2,1)S(1)} %copy-done.1, bf16[16,16,8064]{2,1,0:T(8,128)(2,1)} %pad_maximum_fusion.3.sb, bf16[128,3584]{1,0:T(8,128)(2,1)S(1)} %bitcast.100, bf16[128,3584]{1,0:T(8,128)(2,1)S(1)} %copy-done.9, ...), custom_call_target="tpu_custom_call" | custom-call | tf_op jit(solution)/shard_map/collect/pallas_call | solution.py:337
  386.4 1.1 add_convert_fusion.1
  387.6 1.1 add_convert_fusion
  (59 shorter events, 0.4 us)
Async XLA Ops:
  0.6 220.2 %copy-start = (bf16[1,3584,256]{2,1,0:T(8,128)(2,1)S(1)}, bf16[1,3584,256]{2,1,0:T(8,128)(2,1)}, u32[]{:S(2)}) copy-start(bf16[1,3584,256]{2,1,0:T(8,128)(2,1)} %param.13) | copy-start | bytes 5505028
  4.7 1.2 copy-start.4
  5.8 1.2 copy-start.6
  7.0 1.2 copy-start.7
  194.5 4.3 %copy-start.2 = (bf16[16,16,8064]{2,1,0:T(8,128)(2,1)}, bf16[16,16,8064]{2,1,0:T(8,128)(2,1)S(1)}, u32[]{:S(2)}) copy-start(bf16[16,16,8064]{2,1,0:T(8,128)(2,1)S(1)} %get-tuple-element.11) | copy-start | bytes 12386308
  194.5 4.3 %copy-start.8 = (bf16[128,3584]{1,0:T(8,128)(2,1)}, bf16[128,3584]{1,0:T(8,128)(2,1)S(1)}, u32[]{:S(2)}) copy-start(bf16[128,3584]{1,0:T(8,128)(2,1)S(1)} %get-tuple-element.14.cb) | copy-start | bytes 2752516
  199.7 4.1 %copy-start.10 = (bf16[256,3584]{1,0:T(8,128)(2,1)S(1)}, bf16[256,3584]{1,0:T(8,128)(2,1)}, u32[]{:S(2)}) copy-start(bf16[256,3584]{1,0:T(8,128)(2,1)} %get-tuple-element.40) | copy-start | bytes 5505028
  199.7 4.1 %copy-start.12 = (bf16[256,3584]{1,0:T(8,128)(2,1)S(1)}, bf16[256,3584]{1,0:T(8,128)(2,1)}, u32[]{:S(2)}) copy-start(bf16[256,3584]{1,0:T(8,128)(2,1)} %get-tuple-element.41) | copy-start | bytes 5505028
  201.1 4.1 %copy-start.3 = (bf16[16,16,8064]{2,1,0:T(8,128)(2,1)S(1)}, bf16[16,16,8064]{2,1,0:T(8,128)(2,1)}, u32[]{:S(2)}) copy-start(bf16[16,16,8064]{2,1,0:T(8,128)(2,1)} %copy-done.2) | copy-start | bytes 12386308
  210.0 4.7 %copy-start.17 = (bf16[16,16,8064]{2,1,0:T(8,128)(2,1)S(1)}, bf16[16,16,8064]{2,1,0:T(8,128)(2,1)}, u32[]{:S(2)}) copy-start(bf16[16,16,8064]{2,1,0:T(8,128)(2,1)} %get-tuple-element.13) | copy-start | bytes 12386308
  211.4 0.8 copy-start.18
  220.8 3.5 copy-start.20
  220.8 3.5 copy-start.21
  220.8 3.7 copy-start.22
  226.0 3.0 copy-start.11
  226.0 3.0 copy-start.13
  229.1 3.5 copy-start.15
  229.1 3.4 copy-start.16
  229.1 3.4 copy-start.19
  253.7 4.1 %slice-start.1 = ((bf16[576,3584]{1,0:T(8,128)(2,1)}), bf16[64,3584]{1,0:T(8,128)(2,1)S(1)}, s32[]{:S(2)}) async-start(bf16[576,3584]{1,0:T(8,128)(2,1)} %multiply_convert_fusion.1), calls=%async_computation.1 | async-start | bytes 917504 | tf_op jit(solution)/shard_map/slice | solution.py:382
  260.8 4.9 %copy-start.14 = (bf16[576,3584]{1,0:T(8,128)(2,1)S(1)}, bf16[576,3584]{1,0:T(8,128)(2,1)}, u32[]{:S(2)}) copy-start(bf16[576,3584]{1,0:T(8,128)(2,1)} %fusion.7) | copy-start | bytes 12386308
  264.8 3.0 slice-start
  270.8 4.9 %copy-start.1 = (bf16[16,16,8064]{2,1,0:T(8,128)(2,1)S(1)}, bf16[16,16,8064]{2,1,0:T(8,128)(2,1)}, u32[]{:S(2)}) copy-start(bf16[16,16,8064]{2,1,0:T(8,128)(2,1)} %pad_maximum_fusion.1.sa) | copy-start | bytes 12386308
  270.8 5.2 %copy-start.5 = (bf16[1,128,3584]{2,1,0:T(8,128)(2,1)S(1)}, bf16[1,128,3584]{2,1,0:T(8,128)(2,1)}, u32[]{:S(2)}) copy-start(bf16[1,128,3584]{2,1,0:T(8,128)(2,1)} %param.8) | copy-start | bytes 2752516
  270.8 5.5 %copy-start.9 = (bf16[128,3584]{1,0:T(8,128)(2,1)S(1)}, bf16[128,3584]{1,0:T(8,128)(2,1)}, u32[]{:S(2)}) copy-start(bf16[128,3584]{1,0:T(8,128)(2,1)} %copy-done.8) | copy-start | bytes 2752516

commit v2 on v1

v2 whole, which is shorter than its diff:
```python
import jax
import jax.numpy as jnp
from jax import lax
from jax.experimental import pallas as pl
from jax.experimental.pallas import tpu as pltpu
from jax.sharding import PartitionSpec as P

EPS = 1e-06
MESH = pl.DeviceIdType.MESH
TOK = 128
D = 3584
CAP = 18
EXPERTS = 8
SIDE = 4
PLANE = 16
PARTS = 4
W = D // PARTS
WIDE = 9 * W
HID = 256
TAIL = 4 * PLANE
ROWS = 2 * PLANE * 16 + TAIL
BF = jnp.bfloat16
NEAR = sorted(
    [(i, j) for i in range(SIDE) for j in range(SIDE) if i or j],
    key=lambda s: min(s[0], SIDE - s[0]) + min(s[1], SIDE - s[1]),
)


class Place:
    def __init__(self):
        self.pipe = lax.axis_index("pipe")
        self.expert = lax.axis_index("expert")
        self.half = lax.rem(self.expert, 2)
        self.spot = self.expert // 2
        self.x = self.spot // SIDE
        self.y = lax.rem(self.spot, SIDE)
        self.across = self.expert + 1 - 2 * self.half

    def spot_at(self, dx, dy):
        return lax.rem(self.x + dx, SIDE) * SIDE + lax.rem(self.y + dy, SIDE)

    def plane(self, spot):
        return (self.pipe, spot * 2 + self.half)


def remote(src, dst, send, recv, device):
    return pltpu.make_async_remote_copy(
        src_ref=src, dst_ref=dst, send_sem=send, recv_sem=recv, device_id=device, device_id_type=MESH
    )


def cols(at, width=W):
    return pl.ds(pl.multiple_of(at * W, 128), width)


def part_rows(q):
    return pl.ds(pl.multiple_of(q * W, 128), W)


def rows16(e):
    return pl.ds(pl.multiple_of(e * 16, 16), 16)


def selector(kind, code, part=0):
    row = lax.broadcasted_iota(jnp.int32, (TOK, TOK), 0)
    return ((row == code // 32 * 16 + place(kind, code % 32, part)) & allowed(kind, code % 32)).astype(jnp.float32).astype(BF)


def place(kind, slot, part):
    return {"own0": slot, "own1": slot - 16, "far1": slot + 2, "left": slot - 14 + 4 * part}[kind]


def allowed(kind, slot):
    return {"own0": slot < 16, "own1": slot >= 16, "far1": slot < 14, "left": slot >= 14}[kind]


def unselector(kind, code, part=0):
    lane = lax.broadcasted_iota(jnp.int32, (TOK, PLANE * 16), 1)
    slot = code % 32
    hit = (lane // 32 == code // 32) & (lane % 16 == place(kind, slot, part)) & allowed(kind, slot)
    return hit.astype(jnp.float32).astype(BF)


def fill_selectors(make, sel, t, own_code, far_code):
    sel[t, 0] = make("own0", own_code)
    sel[t, 1] = make("own1", own_code)
    sel[t, 2] = make("far1", far_code)
    for q in range(PARTS):
        sel[t, 3 + q] = make("left", far_code, q)


def dot(a, b):
    return jnp.dot(a, b, preferred_element_type=jnp.float32)


def dot_nt(a, b):
    return lax.dot_general(a, b, (((1,), (1,)), ((), ())), preferred_element_type=jnp.float32)


def dot_tn(a, b):
    return lax.dot_general(a, b, (((0,), (0,)), ((), ())), preferred_element_type=jnp.float32)


def gather_tail(q):
    r = lax.broadcasted_iota(jnp.int32, (TAIL, PLANE * 16), 0)
    c = lax.broadcasted_iota(jnp.int32, (TAIL, PLANE * 16), 1)
    return ((c // 16 == r // 4) & (c % 16 == 4 * q + r % 4)).astype(jnp.float32).astype(BF)


def spread_tail(q):
    c = lax.broadcasted_iota(jnp.int32, (PLANE * 16, TAIL), 0)
    r = lax.broadcasted_iota(jnp.int32, (PLANE * 16, TAIL), 1)
    return ((c // 16 == r // 4) & (c % 16 == 4 * q + r % 4)).astype(jnp.float32).astype(BF)


def span_kernel(
    ax, bx, bc, acode, bcode, acol, bcol, up_in, down_in, column,
    oa, ob, up_out, down_out,
    own_a, far_a, got_b, codes, code_cols, send_a, send_bx, send_bc, ra, rbx, rbc,
    ret_a, ret_b, ga, gb, own, far, up, down, up_grad, down_grad,
    left, sel, sums, tails, tail_ret, hidden, act_grad, act, hid_grad, stat,
    zsend, zrecv, csend, crecv, psend, precv, gsend, grecv, fsend, frecv, local,
):
    me = Place()
    across = (me.pipe, me.across)
    mirror = (7 - me.pipe, me.expert)
    mirror_across = (7 - me.pipe, me.across)
    a_to = lax.rem(me.pipe + 1, 8)
    a_from = lax.rem(me.pipe + 7, 8)
    b_to = lax.rem(8 - me.pipe, 8)
    stays = b_to == me.pipe
    barrier = pltpu.get_barrier_semaphore()
    greet = [me.plane(me.spot_at(i, j)) for i, j in NEAR] + [across, mirror, mirror_across]
    greet += [(a_to, me.expert), (a_to, me.across), (a_from, me.expert), (a_from, me.across), (b_to, me.across)]
    for device in greet:
        pl.semaphore_signal(barrier, inc=1, device_id=device, device_id_type=MESH)

    @pl.when(jnp.logical_not(stays))
    def _():
        pl.semaphore_signal(barrier, inc=1, device_id=(b_to, me.expert), device_id_type=MESH)

    loads = [
        pltpu.make_async_copy(ax, own_a, local.at[0]),
        pltpu.make_async_copy(up_in, up, local.at[1]),
        pltpu.make_async_copy(down_in, down, local.at[2]),
    ]
    for copy in loads:
        copy.start()
    pl.semaphore_wait(barrier, len(greet) + 1 - stays.astype(jnp.int32))

    small = []
    for i, (row, col, to) in enumerate(
        ((acode, acol, across), (bcode, bcol, mirror), (bcode, bcol, mirror_across))
    ):
        small += [
            remote(row, codes.at[i], csend.at[i], crecv.at[i], to),
            remote(col, code_cols.at[i], csend.at[3 + i], crecv.at[3 + i], to),
        ]
    for copy in small:
        copy.start()

    def z_copy(lane, q):
        src, dst, to = [
            (ax, far_a, across),
            (bx, got_b.at[0], mirror),
            (bx, got_b.at[1], mirror_across),
            (bc, got_b.at[2], mirror),
            (bc, got_b.at[3], mirror_across),
        ][lane]
        return remote(src.at[:, cols(q)], dst.at[:, cols(q)], zsend.at[lane, q], zrecv.at[lane, q], to)

    for lanes in ((0,), (1, 2), (3, 4)):
        @pl.loop(0, PARTS)
        def _(q):
            for lane in lanes:
                z_copy(lane, q).start()

    def spread(t, send, recv, at):
        pltpu.make_async_copy(
            send.at[rows16(me.spot // 2), cols(at)], recv.at[me.spot, :, cols(at)], precv.at[t]
        ).start()
        for i, j in NEAR:
            to = me.spot_at(i, j)
            remote(
                send.at[rows16(to // 2), cols(at)], recv.at[me.spot, :, cols(at)],
                psend.at[t], precv.at[t], me.plane(to),
            ).start()

    def spread_back(t, send, recv, at, sem):
        pltpu.make_async_copy(
            send.at[me.spot, :, cols(at)], recv.at[me.spot, :, cols(at)], grecv.at[t, sem]
        ).start()
        for i, j in NEAR:
            to = me.spot_at(i, j)
            remote(
                send.at[to, :, cols(at)], recv.at[me.spot, :, cols(at)],
                gsend.at[t], grecv.at[t, sem], me.plane(to),
            ).start()

    def arrived(ref, sem):
        pltpu.make_async_copy(ref, ref, sem).wait()

    def block(ref, at):
        return ref[:, :, cols(at)].reshape(PLANE * 16, W)

    def put(ref, at, value):
        ref[:, :, cols(at)] = value.reshape(PLANE, 16, W)

    recvs = (ra, rbx, rbc)
    sets = ((0, 256), (256, 256), (512, TAIL))

    def rows_of(t, s, q):
        return block(recvs[t], PARTS * s + q) if s < 2 else tails[t, :, cols(q)]

    def put_rows(t, s, q, value):
        if s < 2:
            put(recvs[t], PARTS * s + q, value)
        else:
            tails[t, :, cols(q)] = value

    def pick_tail(t):
        @pl.loop(0, PARTS)
        def _(q):
            tails[t, :, cols(q)] = dot(gather_tail(q), block(recvs[t], 2 * PARTS)).astype(BF)

    def put_tail(ret):
        left_ret = dot(spread_tail(0), tail_ret[:, cols(0)])
        for q in range(1, PARTS):
            left_ret += dot(spread_tail(q), tail_ret[:, cols(q)])
        put(ret, 2 * PARTS, left_ret.astype(BF))

    def norm_rows(t, s):
        at, n = sets[s]
        rows = pl.ds(at, n)
        stat[0, rows] = jnp.zeros((n, 1), jnp.float32)
        stat[1, rows] = jnp.zeros((n, 1), jnp.float32)
        hidden[rows] = jnp.zeros((n, HID), jnp.float32)

        @pl.loop(0, PARTS)
        def _(q):
            x = rows_of(t, s, q).astype(jnp.float32)
            stat[0, rows] += jnp.sum(x * x, axis=1, keepdims=True)

        stat[0, rows] = lax.rsqrt(stat[0, rows] / D + EPS)

        @pl.loop(0, PARTS)
        def _(q):
            normed = (rows_of(t, s, q).astype(jnp.float32) * stat[0, rows]).astype(BF)
            put_rows(t, s, q, normed)
            hidden[rows] += dot(normed, up[part_rows(q)])
            stat[1, rows] += jnp.sum(normed.astype(jnp.float32) * column[0:1, cols(q)], axis=1, keepdims=True)

        stat[2, rows] = jax.nn.sigmoid(stat[1, rows])

    def forward_rows(s):
        at, n = sets[s]
        rows = pl.ds(at, n)
        norm_rows(0, s)
        h = hidden[rows]
        act[rows] = (h * jax.nn.sigmoid(h)).astype(BF)

        @pl.loop(0, PARTS)
        def _(q):
            value = (stat[2, rows] * dot(act[rows], down[:, cols(q)])).astype(BF)
            if s < 2:
                put(ret_a, PARTS * s + q, value)
            else:
                tail_ret[:, cols(q)] = value

    def gate_rows(s):
        at, n = sets[s]
        rows = pl.ds(at, n)
        act_grad[rows] = jnp.zeros((n, HID), jnp.float32)

        @pl.loop(0, PARTS)
        def _(q):
            cot = (rows_of(2, s, q).astype(jnp.float32) * stat[2, rows]).astype(BF)
            put_rows(2, s, q, cot)
            act_grad[rows] += dot_nt(cot, down[:, cols(q)])

        h, g = hidden[rows], act_grad[rows]
        sig = jax.nn.sigmoid(h)
        a = (h * sig).astype(BF)
        act[rows] = a
        hg = (g * sig * (1.0 + h * (1.0 - sig))).astype(BF)
        hid_grad[rows] = hg
        score_part = jnp.sum(a.astype(jnp.float32) * g, axis=1, keepdims=True) * (1.0 - stat[2, rows])
        stat[3, rows] = score_part
        along = jnp.sum(hg.astype(jnp.float32) * h, axis=1, keepdims=True) + score_part * stat[1, rows]
        stat[4, rows] = along / D

    def back_rows(s, q):
        at, n = sets[s]
        rows = pl.ds(at, n)
        grad = dot_nt(hid_grad[rows], up[part_rows(q)]) + stat[3, rows] * column[0:1, cols(q)]
        value = stat[0, rows] * (grad - rows_of(1, s, q).astype(jnp.float32) * stat[4, rows])
        if s < 2:
            put(ret_b, PARTS * s + q, value.astype(BF))
        else:
            tail_ret[:, cols(q)] = value.astype(BF)

    loads[0].wait()
    sel[0, 0] = selector("own0", acode[0:1, :])

    @pl.loop(0, PARTS)
    def _(q):
        send_a[:, cols(q)] = dot(sel[0, 0], own_a[:, cols(q)]).astype(BF)
        spread(0, send_a, ra, q)

    small[0].wait()
    small[1].wait()
    fill_selectors(selector, sel, 0, acode[0:1, :], codes[0, 0:1, :])
    left[...] = jnp.zeros_like(left)

    @pl.loop(0, PARTS)
    def _(q):
        z_copy(0, q).wait()
        there = far_a[:, cols(q)]
        send_a[:, cols(PARTS + q)] = (dot(sel[0, 1], own_a[:, cols(q)]) + dot(sel[0, 2], there)).astype(BF)
        left[...] += dot(sel[0, 3 + q], there)
        spread(0, send_a, ra, PARTS + q)

    send_a[:, 2 * D:] = left[...].astype(BF)
    spread(0, send_a, ra, 2 * PARTS)

    for copy in small[2:]:
        copy.wait()
    fill_selectors(selector, sel, 1, codes[1, 0:1, :], codes[2, 0:1, :])

    def slot_part(t, send, recv, q):
        z_copy(2 * t - 1, q).wait()
        here = got_b[2 * t - 2, :, cols(q)]
        send[:, cols(q)] = dot(sel[1, 0], here).astype(BF)
        spread(t, send, recv, q)
        z_copy(2 * t, q).wait()
        there = got_b[2 * t - 1, :, cols(q)]
        send[:, cols(PARTS + q)] = (dot(sel[1, 1], here) + dot(sel[1, 2], there)).astype(BF)
        left[...] += dot(sel[1, 3 + q], there)
        spread(t, send, recv, PARTS + q)

    left[...] = jnp.zeros_like(left)

    @pl.loop(0, PARTS)
    def _(q):
        slot_part(1, send_bx, rbx, q)

    send_bx[:, 2 * D:] = left[...].astype(BF)
    spread(1, send_bx, rbx, 2 * PARTS)

    left[...] = jnp.zeros_like(left)
    loads[1].wait()
    loads[2].wait()
    arrived(ra, precv.at[0])
    for q in range(PARTS):
        if q == 0:
            pick_tail(0)
            forward_rows(2)
            put_tail(ret_a)
        if q in (1, 2):
            forward_rows(q - 1)
        slot_part(2, send_bc, rbc, q)
    send_bc[:, 2 * D:] = left[...].astype(BF)
    spread(2, send_bc, rbc, 2 * PARTS)

    spread_back(0, ret_a, ga, 2 * PARTS, PARTS)

    @pl.loop(0, PARTS)
    def _(q):
        spread_back(0, ret_a, ga, PARTS + q, q)
        spread_back(0, ret_a, ga, q, q)

    fill_selectors(unselector, sums, 0, acol[:, 0:1], code_cols[0, :, 0:1])
    fill_selectors(unselector, sums, 1, code_cols[1, :, 0:1], code_cols[2, :, 0:1])

    arrived(rbx, precv.at[1])
    pick_tail(1)
    for s in (2, 0, 1):
        norm_rows(1, s)
    arrived(rbc, precv.at[2])
    pick_tail(2)
    for s in (2, 0, 1):
        gate_rows(s)
        if s == 2:
            @pl.loop(0, PARTS)
            def _(q):
                back_rows(2, q)

            put_tail(ret_b)
            spread_back(1, ret_b, gb, 2 * PARTS, PARTS)

    @pl.loop(0, PARTS)
    def _(q):
        back_rows(1, q)
        spread_back(1, ret_b, gb, PARTS + q, q)
        back_rows(0, q)
        spread_back(1, ret_b, gb, q, q)

    def far_copy(t, out, to, q):
        return remote(
            far.at[t, :, cols(q)], out.at[1, :, cols(q)], fsend.at[t, 1, q], frecv.at[t, 1, q], (to, me.across)
        )

    def own_copy(t, out, to, q):
        return remote(
            own.at[t, :, cols(q)], out.at[0, :, cols(q)], fsend.at[t, 0, q], frecv.at[t, 0, q], (to, me.expert)
        )

    def own_stay(t, out, q):
        return pltpu.make_async_copy(own.at[t, :, cols(q)], out.at[0, :, cols(q)], frecv.at[t, 0, q])

    def collect(t, recv, base, out, to):
        arrived(recv.at[:, :, pl.ds(2 * D, W)], grecv.at[t, PARTS])

        @pl.loop(0, PARTS)
        def _(q):
            arrived(recv.at[:, :, pl.ds(0, 2 * W)], grecv.at[t, q])
            second = block(recv, PARTS + q)
            far[t, :, cols(q)] = (
                dot(sums[t, 2], second) + dot(sums[t, 3 + q], block(recv, 2 * PARTS))
            ).astype(BF)
            far_copy(t, out, to, q).start()
            own[t, :, cols(q)] = (
                base[:, cols(q)].astype(jnp.float32) + dot(sums[t, 0], block(recv, q)) + dot(sums[t, 1], second)
            ).astype(BF)
            if t == 0:
                own_copy(t, out, to, q).start()
            else:
                @pl.when(stays)
                def _():
                    own_stay(t, out, q).start()

                @pl.when(jnp.logical_not(stays))
                def _():
                    own_copy(t, out, to, q).start()

    collect(0, ga, own_a, oa, a_to)

    @pl.loop(0, PARTS)
    def _(q):
        total = dot_tn(act[pl.ds(0, 256)], rows_of(2, 0, q))
        total += dot_tn(act[pl.ds(256, 256)], rows_of(2, 1, q))
        total += dot_tn(act[pl.ds(512, TAIL)], rows_of(2, 2, q))
        down_grad[:, cols(q)] = total.astype(BF)
        total = dot_tn(rows_of(1, 0, q), hid_grad[pl.ds(0, 256)])
        total += dot_tn(rows_of(1, 1, q), hid_grad[pl.ds(256, 256)])
        total += dot_tn(rows_of(1, 2, q), hid_grad[pl.ds(512, TAIL)])
        up_grad[part_rows(q)] = total.astype(BF)

    stores = [
        pltpu.make_async_copy(up_grad, up_out, local.at[3]),
        pltpu.make_async_copy(down_grad, down_out, local.at[4]),
    ]
    for copy in stores:
        copy.start()

    collect(1, gb, got_b.at[2], ob, b_to)

    for t, recv in enumerate(recvs):
        most = recv.at[pl.ds(0, PLANE - 1)]
        remote(most, most, psend.at[t], precv.at[t], across).wait_send()
    for t, recv, out, to in ((0, ga, oa, a_to), (1, gb, ob, b_to)):
        most = recv.at[pl.ds(0, PLANE - 1)]
        remote(most, most, gsend.at[t], grecv.at[t, 0], across).wait_send()

        @pl.loop(0, PARTS)
        def _(q):
            far_copy(t, out, to, q).wait()
            if t == 0:
                own_copy(t, out, to, q).wait()
            else:
                @pl.when(jnp.logical_not(stays))
                def _():
                    own_copy(t, out, to, q).wait()

                @pl.when(stays)
                def _():
                    own_stay(t, out, q).wait()
    for copy in stores:
        copy.wait()


def span(*operands):
    anywhere = pl.BlockSpec(memory_space=pl.ANY)
    inside = pl.BlockSpec(memory_space=pltpu.VMEM)
    dma = pltpu.SemaphoreType.DMA
    pair = jax.ShapeDtypeStruct((2, TOK, D), BF)

    def held(*shape, kind=BF):
        return pltpu.VMEM(shape, kind)

    return pl.pallas_call(
        span_kernel,
        name="span",
        out_shape=(pair, pair, jax.ShapeDtypeStruct((D, HID), BF), jax.ShapeDtypeStruct((HID, D), BF)),
        in_specs=[anywhere] * 3 + [inside] * 4 + [anywhere] * 2 + [inside],
        out_specs=(anywhere,) * 4,
        scratch_shapes=[
            held(TOK, D), held(TOK, D), held(4, TOK, D),
            held(3, 8, TOK, kind=jnp.int32), held(3, TOK, TOK, kind=jnp.int32),
            held(TOK, WIDE), held(TOK, WIDE), held(TOK, WIDE),
            held(PLANE, 16, WIDE), held(PLANE, 16, WIDE), held(PLANE, 16, WIDE),
            held(PLANE, 16, WIDE), held(PLANE, 16, WIDE), held(PLANE, 16, WIDE), held(PLANE, 16, WIDE),
            held(2, TOK, D), held(2, TOK, D), held(D, HID), held(HID, D), held(D, HID), held(HID, D),
            held(TOK, W, kind=jnp.float32), held(2, 3 + PARTS, TOK, TOK), held(2, 3 + PARTS, TOK, PLANE * 16),
            held(3, TAIL, D), held(TAIL, D),
            held(ROWS, HID, kind=jnp.float32), held(ROWS, HID, kind=jnp.float32),
            held(ROWS, HID), held(ROWS, HID), held(5, ROWS, 1, kind=jnp.float32),
            dma((5, PARTS)), dma((5, PARTS)), dma((6,)), dma((6,)), dma((3,)), dma((3,)),
            dma((2,)), dma((2, PARTS + 1)), dma((2, 2, PARTS)), dma((2, 2, PARTS)), dma((5,)),
        ],
        compiler_params=pltpu.CompilerParams(collective_id=1, has_side_effects=True, vmem_limit_bytes=67043328),
    )(*operands)


def slot_code(route):
    ids = route.reshape(TOK)
    same = ids[:, None] == ids[None, :]
    earlier = jnp.arange(TOK)[:, None] < jnp.arange(TOK)[None, :]
    slot = jnp.sum((same & earlier).astype(jnp.int32), axis=0)
    return (ids * 32 + slot).astype(jnp.int32)


def body(a_input, a_route, b_saved, b_grad, b_route, up_weight, down_weight, router):
    group = lax.axis_size("expert") // EXPERTS
    mine = lax.axis_index("expert") // group
    column = lax.dynamic_slice(router[0], (0, mine), (D, 1))[:, 0].astype(jnp.float32)
    codes = [slot_code(a_route[0]), slot_code(b_route[0])]
    out_a, out_b, up_grad, down_grad = span(
        a_input[0], b_saved[0], b_grad[0],
        *[jnp.broadcast_to(c[None, :], (8, TOK)) for c in codes],
        *[jnp.broadcast_to(c[:, None], (TOK, TOK)) for c in codes],
        up_weight[0], down_weight[0], jnp.broadcast_to(column[None, :], (8, D)),
    )
    a_next = (out_a[0].astype(jnp.float32) + out_a[1].astype(jnp.float32)).astype(BF)
    b_next = (out_b[0].astype(jnp.float32) + out_b[1].astype(jnp.float32)).astype(BF)
    return a_next[None], b_next[None], up_grad[None], down_grad[None]


def solution(mesh):
    rows = P("pipe", "expert", None)
    return jax.shard_map(
        body,
        mesh=mesh,
        in_specs=(rows, rows, rows, rows, rows, P("pipe", None, "expert"), rows, P("pipe", None, None)),
        out_specs=(rows, rows, P("pipe", None, "expert"), rows),
        check_vma=False,
    )
```

time: 389 us -> 307 us (0.79)
  local copies, waits for them, and re-layouts: 35.8 us -> 6.66 us
  other arithmetic: 31.6 us -> 7.64 us
  matrix products: 23.7 us -> 0 us
  Pallas kernels: 297 us -> 291 us
    dot_general x6 -> x0, matrix products: 23.7 us -> none  [mm(): lax.dot_general(a, b, (((ca,), (cb,)), ((), ())), preferred_element_type=...]
    slice x12 -> x0, local copies, waits for them, and re-layouts: 14.2 us -> none  [the longest x3 6.4 us: to_rows(): return jnp.concatenate([flat[:, :D], flat[:, D:2 * D], tail], axis=0)]
    reshape x9 -> x0, local copies, waits for them, and re-layouts: 11.5 us -> none  [the longest x5 7.36 us: to_rows(): flat[:, 2 * D:].reshape(PLANE, PARTS, 4, W).transpose(0, 2, 1, 3)]
    convert_element_type x2 -> x0, other arithmetic: 10 us -> none  [the longest x1 8.9 us: body(): (scale * grad - x * (scale * scale * scale) * along / D).astype(BF)]
    concatenate x2 -> x0, other arithmetic: 7.92 us -> none  [from_rows(): jnp.concatenate([rows[:n], rows[n:2 * n], tail], axis=1)]
    reduce_sum x3 -> x0, other arithmetic: 6.56 us -> none  [the longest x2 5.16 us: plan(): scale = lax.rsqrt(jnp.mean(x * x, axis=1, keepdims=True) + EPS)]
    pallas_call x2 -> x1, Pallas kernels: 297 us -> 291 us  [span(): pl.pallas_call(span_kernel, name='span', out_shape=(pair, pair, jax.Shape...]
where the time goes in v2:
time: 307 us; the launch traced here: 306 us
  Pallas kernels  291 us (95%)
  other arithmetic  7.64 us (2%)
  local copies, waits for them, and re-layouts  6.66 us (2%)
    pallas_call x1, Pallas kernels, span(): pl.pallas_call(span_kernel, name='span', out_shape=(pair, pair, jax.Shape...  291 us

profile of v2, /device:TPU:92, one launch (start us, length us, event | category | flops | bytes accessed | tf_op | source)
XLA Modules:
  0.0 305.6 jit_solution(16868203095252353397)
XLA Ops:
  0.6 0.8 convert_reduce_fusion
  1.5 0.7 multiply_add_fusion
  2.1 0.8 convert_reduce_fusion.1
  3.0 0.7 multiply_add_fusion.1
  3.6 0.6 broadcast_in_dim.14.acode
  4.2 0.6 broadcast_in_dim.15.bcode
  4.8 0.9 convert_reduce_fusion.2
  5.7 0.7 broadcast_in_dim.17.bcol
  6.4 0.7 broadcast_in_dim.16.acol
  7.1 0.7 broadcast_in_dim.18.column
  7.8 290.7 %span.1 = (bf16[2,128,3584]{2,1,0:T(8,128)(2,1)}, bf16[2,128,3584]{2,1,0:T(8,128)(2,1)}, bf16[3584,256]{1,0:T(8,128)(2,1)}, bf16[256,3584]{1,0:T(8,128)(2,1)}) custom-call(bf16[128,3584]{1,0:T(8,128)(2,1)} %bitcast.15, bf16[128,3584]{1,0:T(8,128)(2,1)} %bitcast.16, bf16[128,3584]{1,0:T(8,128)(2,1)} %bitcast.17, s32[8,128]{1,0:T(8,128)} %broadcast_in_dim.14.acode, ...), custom_call_target="tpu_custom_call" | custom-call | tf_op jit(solution)/shard_map/span/pallas_call | solution.py:491
  298.4 0.0 copy-start.1
  298.4 3.8 %add_convert_fusion = (bf16[1,128,3584]{2,1,0:T(8,128)(2,1)}, bf16[1,128,3584]{2,1,0:T(8,128)(2,1)}) fusion(bf16[2,128,3584]{2,1,0:T(8,128)(2,1)} %get-tuple-element.9, bf16[2,128,3584]{2,1,0:T(8,128)(2,1)} %get-tuple-element.8), kind=kLoop, calls=%fused_computation | loop fusion | flops 3670016 | bytes 5505024 | tf_op jit(solution)/shard_map/convert_element_type | solution.py:535
  302.2 0.0 copy-done.1
  302.2 0.0 copy-start
  302.2 1.2 copy.14
  303.5 0.9 copy-done
  304.4 1.2 copy.15
Async XLA Ops:
  298.4 3.8 %copy-start.1 = (bf16[3584,256]{1,0:T(8,128)(2,1)S(1)}, bf16[3584,256]{1,0:T(8,128)(2,1)}, u32[]{:S(2)}) copy-start(bf16[3584,256]{1,0:T(8,128)(2,1)} %get-tuple-element.10) | copy-start | bytes 5505028
  302.2 2.2 copy-start

commit v3 on v2

v3 whole, which is shorter than its diff:
```python
import jax
import jax.numpy as jnp
from jax import lax
from jax.experimental import pallas as pl
from jax.experimental.pallas import tpu as pltpu
from jax.sharding import PartitionSpec as P

EPS = 1e-06
MESH = pl.DeviceIdType.MESH
TOK = 128
D = 3584
CAP = 18
EXPERTS = 8
SIDE = 4
GROUP = 8
PARTS = 4
W = D // PARTS
WIDE = 9 * W
HALF = 256
HID = 2 * HALF
LINES = GROUP * 16
TAIL = GROUP * 4
ROWS = 2 * LINES + TAIL
BF = jnp.bfloat16
NEAR = sorted(
    [(i, j) for i in range(SIDE) for j in range(2) if i or j], key=lambda s: min(s[0], SIDE - s[0]) + s[1]
)


class Place:
    def __init__(self):
        self.pipe = lax.axis_index("pipe")
        self.expert = lax.axis_index("expert")
        self.half = lax.rem(self.expert, 2)
        self.x = self.expert // 8
        self.y = lax.rem(self.expert // 2, SIDE)
        self.across = self.expert + 1 - 2 * self.half
        self.mine = self.expert // 4
        self.twin = (self.pipe, self.expert + 2 - 4 * lax.rem(self.y, 2))

    def peer(self, dx, flip):
        x = lax.rem(self.x + dx, SIDE)
        y = 3 - self.y if flip else self.y
        return x, x * 2 + y // 2, (self.pipe, x * 8 + y * 2 + self.half)


def remote(src, dst, send, recv, device):
    return pltpu.make_async_remote_copy(
        src_ref=src, dst_ref=dst, send_sem=send, recv_sem=recv, device_id=device, device_id_type=MESH
    )


def cols(at, width=W):
    return pl.ds(pl.multiple_of(at * W, 128), width)


def part_rows(q):
    return pl.ds(pl.multiple_of(q * W, 128), W)


def rows16(e):
    return pl.ds(pl.multiple_of(e * 16, 16), 16)


def selector(kind, code, part=0):
    row = lax.broadcasted_iota(jnp.int32, (TOK, TOK), 0)
    return ((row == code // 32 * 16 + place(kind, code % 32, part)) & allowed(kind, code % 32)).astype(jnp.float32).astype(BF)


def place(kind, slot, part):
    return {"own0": slot, "own1": slot - 16, "far1": slot + 2, "left": slot - 14 + 4 * part}[kind]


def allowed(kind, slot):
    return {"own0": slot < 16, "own1": slot >= 16, "far1": slot < 14, "left": slot >= 14}[kind]


def unselector(kind, code, part=0):
    lane = lax.broadcasted_iota(jnp.int32, (TOK, LINES), 1)
    slot = code % 32
    hit = (lane // 16 == code // 32) & (lane % 16 == place(kind, slot, part)) & allowed(kind, slot)
    return hit.astype(jnp.float32).astype(BF)


def fill_selectors(make, sel, t, own_code, far_code):
    sel[t, 0] = make("own0", own_code)
    sel[t, 1] = make("own1", own_code)
    sel[t, 2] = make("far1", far_code)
    for q in range(PARTS):
        sel[t, 3 + q] = make("left", far_code, q)


def codes_of(ids):
    i = lax.broadcasted_iota(jnp.int32, (TOK, TOK), 0)
    j = lax.broadcasted_iota(jnp.int32, (TOK, TOK), 1)
    wide = jnp.broadcast_to(ids, (TOK, TOK))
    col = jnp.sum(jnp.where(i == j, wide, 0).astype(jnp.float32), axis=1, keepdims=True).astype(jnp.int32)
    same = col == wide
    slot_row = jnp.sum(jnp.where(same & (i < j), 1.0, 0.0), axis=0, keepdims=True).astype(jnp.int32)
    slot_col = jnp.sum(jnp.where(same & (j < i), 1.0, 0.0), axis=1, keepdims=True).astype(jnp.int32)
    return ids * 32 + slot_row, col * 32 + slot_col


def dot(a, b):
    return jnp.dot(a, b, preferred_element_type=jnp.float32)


def dot_nt(a, b):
    return lax.dot_general(a, b, (((1,), (1,)), ((), ())), preferred_element_type=jnp.float32)


def dot_tn(a, b):
    return lax.dot_general(a, b, (((0,), (0,)), ((), ())), preferred_element_type=jnp.float32)


def gather_tail(q):
    r = lax.broadcasted_iota(jnp.int32, (TAIL, LINES), 0)
    c = lax.broadcasted_iota(jnp.int32, (TAIL, LINES), 1)
    return ((c // 16 == r // 4) & (c % 16 == 4 * q + r % 4)).astype(jnp.float32).astype(BF)


def spread_tail(q):
    c = lax.broadcasted_iota(jnp.int32, (LINES, TAIL), 0)
    r = lax.broadcasted_iota(jnp.int32, (LINES, TAIL), 1)
    return ((c // 16 == r // 4) & (c % 16 == 4 * q + r % 4)).astype(jnp.float32).astype(BF)


def span_kernel(
    ax, bx, bc, a_ids, b_ids, up_in, down_in, column,
    oa, ob, up_out, down_out,
    own_a, far_a, got_b, ids, send_a, send_bx, send_bc, ra, rbx, rbc,
    ret_a, ret_b, ga, gb, own, far, up, down, up_own, up_far, down_own, down_far,
    left, sel, sums, tails, tail_ret, hidden, act_grad, act, act_a, hid_grad, stat,
    zsend, zrecv, csend, crecv, psend, precv, gsend, grecv, fsend, frecv, wsend, wrecv, dsend, drecv, local,
):
    me = Place()
    across = (me.pipe, me.across)
    mirror = (7 - me.pipe, me.expert)
    mirror_across = (7 - me.pipe, me.across)
    a_to = lax.rem(me.pipe + 1, 8)
    a_from = lax.rem(me.pipe + 7, 8)
    b_to = lax.rem(8 - me.pipe, 8)
    stays = b_to == me.pipe
    barrier = pltpu.get_barrier_semaphore()
    greet = [me.peer(i, j)[2] for i, j in NEAR] + [me.twin, across, mirror, mirror_across]
    greet += [(a_to, me.expert), (a_to, me.across), (a_from, me.expert), (a_from, me.across), (b_to, me.across)]
    for device in greet:
        pl.semaphore_signal(barrier, inc=1, device_id=device, device_id_type=MESH)

    @pl.when(jnp.logical_not(stays))
    def _():
        pl.semaphore_signal(barrier, inc=1, device_id=(b_to, me.expert), device_id_type=MESH)

    loads = [
        pltpu.make_async_copy(ax, own_a, local.at[0]),
        pltpu.make_async_copy(up_in, up.at[:, pl.ds(0, HALF)], local.at[1]),
        pltpu.make_async_copy(down_in, down.at[pl.ds(0, HALF)], local.at[2]),
    ]
    for copy in loads:
        copy.start()
    pl.semaphore_wait(barrier, len(greet) + 1 - stays.astype(jnp.int32))

    small = [
        remote(src, ids.at[i], csend.at[i], crecv.at[i], to)
        for i, (src, to) in enumerate(((a_ids, across), (b_ids, mirror), (b_ids, mirror_across)))
    ]
    weights = [
        remote(up_in, up.at[:, pl.ds(HALF, HALF)], wsend.at[0], wrecv.at[0], me.twin),
        remote(down_in, down.at[pl.ds(HALF, HALF)], wsend.at[1], wrecv.at[1], me.twin),
    ]
    for copy in small + weights:
        copy.start()

    def z_copy(lane, q):
        src, dst, to = [
            (ax, far_a, across),
            (bx, got_b.at[0], mirror),
            (bx, got_b.at[1], mirror_across),
            (bc, got_b.at[2], mirror),
            (bc, got_b.at[3], mirror_across),
        ][lane]
        return remote(src.at[:, cols(q)], dst.at[:, cols(q)], zsend.at[lane, q], zrecv.at[lane, q], to)

    for lanes in ((1, 2), (3, 4), (0,)):
        @pl.loop(0, PARTS)
        def _(q):
            for lane in lanes:
                z_copy(lane, q).start()

    def spread(t, send, recv, at):
        pltpu.make_async_copy(
            send.at[rows16(me.mine), cols(at)], recv.at[me.x * 2, :, cols(at)], precv.at[t]
        ).start()
        for i, j in NEAR:
            x, e, device = me.peer(i, j)
            remote(
                send.at[rows16(e), cols(at)], recv.at[me.x * 2 + j, :, cols(at)], psend.at[t], precv.at[t], device
            ).start()

    def spread_back(t, send, recv, at, sem):
        pltpu.make_async_copy(
            send.at[me.x * 2, :, cols(at)], recv.at[me.mine, :, cols(at)], grecv.at[t, sem]
        ).start()
        for i, j in NEAR:
            x, e, device = me.peer(i, j)
            remote(
                send.at[x * 2 + j, :, cols(at)], recv.at[me.mine, :, cols(at)], gsend.at[t], grecv.at[t, sem], device
            ).start()

    def arrived(ref, sem):
        pltpu.make_async_copy(ref, ref, sem).wait()

    def block(ref, at):
        return ref[:, :, cols(at)].reshape(LINES, W)

    def put(ref, at, value):
        ref[:, :, cols(at)] = value.reshape(GROUP, 16, W)

    recvs = (ra, rbx, rbc)
    sets = ((0, LINES), (LINES, LINES), (2 * LINES, TAIL))

    def rows_of(t, s, q):
        return block(recvs[t], PARTS * s + q) if s < 2 else tails[t, :, cols(q)]

    def put_rows(t, s, q, value):
        if s < 2:
            put(recvs[t], PARTS * s + q, value)
        else:
            tails[t, :, cols(q)] = value

    def pick_tail(t):
        @pl.loop(0, PARTS)
        def _(q):
            tails[t, :, cols(q)] = dot(gather_tail(q), block(recvs[t], 2 * PARTS)).astype(BF)

    def put_tail(ret):
        left_ret = dot(spread_tail(0), tail_ret[:, cols(0)])
        for q in range(1, PARTS):
            left_ret += dot(spread_tail(q), tail_ret[:, cols(q)])
        put(ret, 2 * PARTS, left_ret.astype(BF))

    def norm_rows(t, s):
        at, n = sets[s]
        rows = pl.ds(at, n)
        stat[0, rows] = jnp.zeros((n, 1), jnp.float32)
        stat[1, rows] = jnp.zeros((n, 1), jnp.float32)
        hidden[rows] = jnp.zeros((n, HID), jnp.float32)

        @pl.loop(0, PARTS)
        def _(q):
            x = rows_of(t, s, q).astype(jnp.float32)
            stat[0, rows] += jnp.sum(x * x, axis=1, keepdims=True)

        stat[0, rows] = lax.rsqrt(stat[0, rows] / D + EPS)

        @pl.loop(0, PARTS)
        def _(q):
            normed = (rows_of(t, s, q).astype(jnp.float32) * stat[0, rows]).astype(BF)
            put_rows(t, s, q, normed)
            hidden[rows] += dot(normed, up[part_rows(q)])
            stat[1, rows] += jnp.sum(normed.astype(jnp.float32) * column[0:1, cols(q)], axis=1, keepdims=True)

        stat[2, rows] = jax.nn.sigmoid(stat[1, rows])

    def forward_rows(s):
        at, n = sets[s]
        rows = pl.ds(at, n)
        norm_rows(0, s)
        h = hidden[rows]
        act_a[rows] = (h * jax.nn.sigmoid(h)).astype(BF)

    def out_rows(s, q):
        at, n = sets[s]
        rows = pl.ds(at, n)
        value = (stat[2, rows] * dot(act_a[rows], down[:, cols(q)])).astype(BF)
        if s < 2:
            put(ret_a, PARTS * s + q, value)
        else:
            tail_ret[:, cols(q)] = value

    def gate_rows(s):
        at, n = sets[s]
        rows = pl.ds(at, n)
        act_grad[rows] = jnp.zeros((n, HID), jnp.float32)

        @pl.loop(0, PARTS)
        def _(q):
            cot = (rows_of(2, s, q).astype(jnp.float32) * stat[2, rows]).astype(BF)
            put_rows(2, s, q, cot)
            act_grad[rows] += dot_nt(cot, down[:, cols(q)])

        h, g = hidden[rows], act_grad[rows]
        sig = jax.nn.sigmoid(h)
        a = (h * sig).astype(BF)
        act[rows] = a
        hg = (g * sig * (1.0 + h * (1.0 - sig))).astype(BF)
        hid_grad[rows] = hg
        score_part = jnp.sum(a.astype(jnp.float32) * g, axis=1, keepdims=True) * (1.0 - stat[2, rows])
        stat[3, rows] = score_part
        along = jnp.sum(hg.astype(jnp.float32) * h, axis=1, keepdims=True) + score_part * stat[1, rows]
        stat[4, rows] = along / D

    def back_rows(s, q):
        at, n = sets[s]
        rows = pl.ds(at, n)
        grad = dot_nt(hid_grad[rows], up[part_rows(q)]) + stat[3, rows] * column[0:1, cols(q)]
        value = stat[0, rows] * (grad - rows_of(1, s, q).astype(jnp.float32) * stat[4, rows])
        if s < 2:
            put(ret_b, PARTS * s + q, value.astype(BF))
        else:
            tail_ret[:, cols(q)] = value.astype(BF)

    def far_copy(t, out, to, q):
        return remote(
            far.at[t, :, cols(q)], out.at[1, :, cols(q)], fsend.at[t, 1, q], frecv.at[t, 1, q], (to, me.across)
        )

    def own_copy(t, out, to, q):
        return remote(
            own.at[t, :, cols(q)], out.at[0, :, cols(q)], fsend.at[t, 0, q], frecv.at[t, 0, q], (to, me.expert)
        )

    def own_stay(t, out, q):
        return pltpu.make_async_copy(own.at[t, :, cols(q)], out.at[0, :, cols(q)], frecv.at[t, 0, q])

    ends = ((ga, own_a, oa, a_to), (gb, got_b.at[2], ob, b_to))

    def collect_edge(t):
        arrived(ends[t][0].at[:, :, pl.ds(2 * D, W)], grecv.at[t, PARTS])

    def collect(t, q):
        recv, base, out, to = ends[t]
        arrived(recv.at[:, :, pl.ds(0, 2 * W)], grecv.at[t, q])
        second = block(recv, PARTS + q)
        far[t, :, cols(q)] = (dot(sums[t, 2], second) + dot(sums[t, 3 + q], block(recv, 2 * PARTS))).astype(BF)
        far_copy(t, out, to, q).start()
        own[t, :, cols(q)] = (
            base[:, cols(q)].astype(jnp.float32) + dot(sums[t, 0], block(recv, q)) + dot(sums[t, 1], second)
        ).astype(BF)
        if t == 0:
            own_copy(t, out, to, q).start()
        else:
            @pl.when(stays)
            def _():
                own_stay(t, out, q).start()

            @pl.when(jnp.logical_not(stays))
            def _():
                own_copy(t, out, to, q).start()

    def down_part(at, q):
        total = 0.0
        for s, (first, n) in enumerate(sets):
            total += dot_tn(act[pl.ds(first, n), pl.ds(at, HALF)], rows_of(2, s, q))
        return total.astype(BF)

    def up_part(at, q):
        total = 0.0
        for s, (first, n) in enumerate(sets):
            total += dot_tn(rows_of(1, s, q), hid_grad[pl.ds(first, n), pl.ds(at, HALF)])
        return total.astype(BF)

    def grad_copies(q):
        return [
            remote(down_far.at[:, cols(q)], down_out.at[1, :, cols(q)], dsend.at[0, q], drecv.at[0, q], me.twin),
            remote(up_far.at[part_rows(q)], up_out.at[1, part_rows(q)], dsend.at[1, q], drecv.at[1, q], me.twin),
        ]

    a_row, a_col = codes_of(a_ids[...])
    sel[0, 0] = selector("own0", a_row)
    loads[0].wait()

    @pl.loop(0, PARTS)
    def _(q):
        send_a[:, cols(q)] = dot(sel[0, 0], own_a[:, cols(q)]).astype(BF)
        spread(0, send_a, ra, q)

    for copy in small:
        copy.wait()
    b_row, b_col = codes_of(ids[1])
    b_far_row, b_far_col = codes_of(ids[2])
    fill_selectors(selector, sel, 1, b_row, b_far_row)

    for t, send, recv in ((1, send_bx, rbx), (2, send_bc, rbc)):
        left[...] = jnp.zeros_like(left)

        @pl.loop(0, PARTS)
        def _(q):
            z_copy(2 * t - 1, q).wait()
            here = got_b[2 * t - 2, :, cols(q)]
            send[:, cols(q)] = dot(sel[1, 0], here).astype(BF)
            spread(t, send, recv, q)
            z_copy(2 * t, q).wait()
            there = got_b[2 * t - 1, :, cols(q)]
            send[:, cols(PARTS + q)] = (dot(sel[1, 1], here) + dot(sel[1, 2], there)).astype(BF)
            left[...] += dot(sel[1, 3 + q], there)
            spread(t, send, recv, PARTS + q)

        send[:, 2 * D:] = left[...].astype(BF)
        spread(t, send, recv, 2 * PARTS)
        if t == 1:
            a_far_row, a_far_col = codes_of(ids[0])
            fill_selectors(selector, sel, 0, a_row, a_far_row)
            fill_selectors(unselector, sums, 0, a_col, a_far_col)
            fill_selectors(unselector, sums, 1, b_col, b_far_col)

    for copy in loads[1:] + weights:
        copy.wait()
    arrived(rbx, precv.at[1])
    pick_tail(1)
    for s in (2, 0, 1):
        norm_rows(1, s)
    arrived(rbc, precv.at[2])
    pick_tail(2)
    for s in (2, 0, 1):
        gate_rows(s)
        if s == 2:
            @pl.loop(0, PARTS)
            def _(q):
                back_rows(2, q)

            put_tail(ret_b)
            spread_back(1, ret_b, gb, 2 * PARTS, PARTS)

    @pl.loop(0, PARTS)
    def _(q):
        back_rows(1, q)
        spread_back(1, ret_b, gb, PARTS + q, q)
        back_rows(0, q)
        spread_back(1, ret_b, gb, q, q)

    @pl.loop(0, PARTS)
    def _(q):
        down_far[:, cols(q)] = down_part(HALF, q)
        up_far[part_rows(q)] = up_part(HALF, q)
        for copy in grad_copies(q):
            copy.start()

    left[...] = jnp.zeros_like(left)
    for q in range(PARTS):
        if q == PARTS - 1:
            collect_edge(1)
            collect(1, 0)
        z_copy(0, q).wait()
        there = far_a[:, cols(q)]
        send_a[:, cols(PARTS + q)] = (dot(sel[0, 1], own_a[:, cols(q)]) + dot(sel[0, 2], there)).astype(BF)
        left[...] += dot(sel[0, 3 + q], there)
        spread(0, send_a, ra, PARTS + q)

    send_a[:, 2 * D:] = left[...].astype(BF)
    spread(0, send_a, ra, 2 * PARTS)

    @pl.loop(1, PARTS)
    def _(q):
        collect(1, q)

    arrived(ra, precv.at[0])
    pick_tail(0)
    forward_rows(2)

    @pl.loop(0, PARTS)
    def _(q):
        out_rows(2, q)

    put_tail(ret_a)
    spread_back(0, ret_a, ga, 2 * PARTS, PARTS)
    forward_rows(1)
    forward_rows(0)

    @pl.loop(0, PARTS)
    def _(q):
        out_rows(1, q)
        spread_back(0, ret_a, ga, PARTS + q, q)
        out_rows(0, q)
        spread_back(0, ret_a, ga, q, q)

    @pl.loop(0, PARTS)
    def _(q):
        down_own[:, cols(q)] = down_part(0, q)
        up_own[part_rows(q)] = up_part(0, q)

    stores = [
        pltpu.make_async_copy(up_own, up_out.at[0], local.at[3]),
        pltpu.make_async_copy(down_own, down_out.at[0], local.at[4]),
    ]
    for copy in stores:
        copy.start()

    collect_edge(0)

    @pl.loop(0, PARTS)
    def _(q):
        collect(0, q)

    for t, recv in enumerate(recvs):
        most = recv.at[pl.ds(0, GROUP - 1)]
        remote(most, most, psend.at[t], precv.at[t], across).wait_send()
    for t, (recv, base, out, to) in enumerate(ends):
        most = recv.at[pl.ds(0, GROUP - 1)]
        remote(most, most, gsend.at[t], grecv.at[t, 0], across).wait_send()

        @pl.loop(0, PARTS)
        def _(q):
            far_copy(t, out, to, q).wait()
            if t == 0:
                own_copy(t, out, to, q).wait()
                for copy in grad_copies(q):
                    copy.wait()
            else:
                @pl.when(jnp.logical_not(stays))
                def _():
                    own_copy(t, out, to, q).wait()

                @pl.when(stays)
                def _():
                    own_stay(t, out, q).wait()
    for copy in stores:
        copy.wait()


def span(*operands):
    anywhere = pl.BlockSpec(memory_space=pl.ANY)
    inside = pl.BlockSpec(memory_space=pltpu.VMEM)
    dma = pltpu.SemaphoreType.DMA
    pair = jax.ShapeDtypeStruct((2, TOK, D), BF)

    def held(*shape, kind=BF):
        return pltpu.VMEM(shape, kind)

    def block_of():
        return held(GROUP, 16, WIDE)

    return pl.pallas_call(
        span_kernel,
        name="span",
        out_shape=(
            pair, pair, jax.ShapeDtypeStruct((2, D, HALF), BF), jax.ShapeDtypeStruct((2, HALF, D), BF)
        ),
        in_specs=[anywhere] * 3 + [inside] * 2 + [anywhere] * 2 + [inside],
        out_specs=(anywhere,) * 4,
        scratch_shapes=[
            held(TOK, D), held(TOK, D), held(4, TOK, D), held(3, 1, TOK, kind=jnp.int32),
            held(TOK, WIDE), held(TOK, WIDE), held(TOK, WIDE), *[block_of() for _ in range(7)],
            held(2, TOK, D), held(2, TOK, D), held(D, HID), held(HID, D),
            held(D, HALF), held(D, HALF), held(HALF, D), held(HALF, D),
            held(TOK, W, kind=jnp.float32), held(2, 3 + PARTS, TOK, TOK), held(2, 3 + PARTS, TOK, LINES),
            held(3, TAIL, D), held(TAIL, D),
            held(ROWS, HID, kind=jnp.float32), held(ROWS, HID, kind=jnp.float32),
            held(ROWS, HID), held(ROWS, HID), held(ROWS, HID), held(5, ROWS, 1, kind=jnp.float32),
            dma((5, PARTS)), dma((5, PARTS)), dma((3,)), dma((3,)), dma((3,)), dma((3,)),
            dma((2,)), dma((2, PARTS + 1)), dma((2, 2, PARTS)), dma((2, 2, PARTS)),
            dma((2,)), dma((2,)), dma((2, PARTS)), dma((2, PARTS)), dma((5,)),
        ],
        compiler_params=pltpu.CompilerParams(collective_id=1, has_side_effects=True, vmem_limit_bytes=67043328),
    )(*operands)


def add_pair(pair):
    return (pair[0].astype(jnp.float32) + pair[1].astype(jnp.float32)).astype(BF)[None]


def body(a_input, a_route, b_saved, b_grad, b_route, up_weight, down_weight, router):
    group = lax.axis_size("expert") // EXPERTS
    mine = lax.axis_index("expert") // group
    column = lax.dynamic_slice(router[0], (0, mine), (D, 1)).reshape(1, D).astype(jnp.float32)
    out_a, out_b, up_grad, down_grad = span(
        a_input[0], b_saved[0], b_grad[0], a_route.reshape(1, TOK), b_route.reshape(1, TOK),
        up_weight[0], down_weight[0], column,
    )
    return add_pair(out_a), add_pair(out_b), add_pair(up_grad), add_pair(down_grad)


def solution(mesh):
    rows = P("pipe", "expert", None)
    return jax.shard_map(
        body,
        mesh=mesh,
        in_specs=(rows, rows, rows, rows, rows, P("pipe", None, "expert"), rows, P("pipe", None, None)),
        out_specs=(rows, rows, P("pipe", None, "expert"), rows),
        check_vma=False,
    )
```

time: 307 us -> 237 us (0.77)
  the two profiles are of different devices: /device:TPU:92 before, /device:TPU:33 now
where the time goes in v3:
time: 237 us; the launch traced here: 236 us
  Pallas kernels  226 us (95%)
  other arithmetic  8.69 us (4%)
    pallas_call x1, Pallas kernels, span(): pl.pallas_call(span_kernel, name='span', out_shape=(pair, pair, jax.Shape...  226 us
    convert_element_type x3, other arithmetic, add_pair(): (pair[0].astype(jnp.float32) + pair[1].astype(jnp.float32)).astype(BF)[None]  7.25 us

profile of v3, /device:TPU:33, one launch (start us, length us, event | category | flops | bytes accessed | tf_op | source)
XLA Modules:
  0.0 236.5 jit_solution(3312889790102943562)
XLA Ops:
  0.6 1.4 bitcast_convert_fusion.column
  2.1 226.2 %span.1 = (bf16[2,128,3584]{2,1,0:T(8,128)(2,1)}, bf16[2,128,3584]{2,1,0:T(8,128)(2,1)}, bf16[2,3584,256]{2,1,0:T(8,128)(2,1)}, bf16[2,256,3584]{2,1,0:T(8,128)(2,1)}) custom-call(bf16[128,3584]{1,0:T(8,128)(2,1)} %bitcast.12, bf16[128,3584]{1,0:T(8,128)(2,1)} %bitcast.13, bf16[128,3584]{1,0:T(8,128)(2,1)} %bitcast.14, s32[1,128]{1,0:T(1,128)} %bitcast.15, ...), custom_call_target="tpu_custom_call" | custom-call | tf_op jit(solution)/shard_map/span/pallas_call | solution.py:533
  228.3 0.0 copy-start.1
  228.3 3.8 %add_convert_fusion.2 = (bf16[1,128,3584]{2,1,0:T(8,128)(2,1)}, bf16[1,128,3584]{2,1,0:T(8,128)(2,1)}) fusion(bf16[2,128,3584]{2,1,0:T(8,128)(2,1)} %get-tuple-element.9, bf16[2,128,3584]{2,1,0:T(8,128)(2,1)} %get-tuple-element.8), kind=kLoop, calls=%fused_computation.2 | loop fusion | flops 3670016 | bytes 5505024 | tf_op jit(solution)/shard_map/convert_element_type | solution.py:559
  232.1 0.0 copy-done.1
  232.1 0.0 copy-start
  232.1 1.8 add_convert_fusion.1
  233.9 0.9 copy-done
  234.8 1.7 add_convert_fusion
Async XLA Ops:
  228.3 3.8 %copy-start.1 = (bf16[2,3584,256]{2,1,0:T(8,128)(2,1)S(1)}, bf16[2,3584,256]{2,1,0:T(8,128)(2,1)}, u32[]{:S(2)}) copy-start(bf16[2,3584,256]{2,1,0:T(8,128)(2,1)} %get-tuple-element.10) | copy-start | bytes 11010052
  232.1 2.7 %copy-start = (bf16[2,256,3584]{2,1,0:T(8,128)(2,1)S(1)}, bf16[2,256,3584]{2,1,0:T(8,128)(2,1)}, u32[]{:S(2)}) copy-start(bf16[2,256,3584]{2,1,0:T(8,128)(2,1)} %get-tuple-element.11) | copy-start | bytes 11010052

commit v4 on v3

--- a/solution.py
+++ b/solution.py
@@ -129,9 +129,9 @@
     ax, bx, bc, a_ids, b_ids, up_in, down_in, column,
     oa, ob, up_out, down_out,
     own_a, far_a, got_b, ids, send_a, send_bx, send_bc, ra, rbx, rbc,
-    ret_a, ret_b, ga, gb, own, far, up, down, up_own, up_far, down_own, down_far,
-    left, sel, sums, tails, tail_ret, hidden, act_grad, act, act_a, hid_grad, stat,
-    zsend, zrecv, csend, crecv, psend, precv, gsend, grecv, fsend, frecv, wsend, wrecv, dsend, drecv, local,
+    ret_a, ret_b, ga, gb, own, far, fin, up, down, up_got, up_far, down_got, down_far,
+    left, sel, sums, tails, tail_ret, hidden, hidden_a, act_grad, act, act_a, hid_grad, stat, stat_a,
+    zsend, zrecv, csend, crecv, psend, precv, gsend, grecv, fsend, frecv, wsend, wrecv, dsend, drecv, out_sem, local,
 ):
     me = Place()
     across = (me.pipe, me.across)
@@ -187,14 +187,13 @@
             for lane in lanes:
                 z_copy(lane, q).start()
 
-    def spread(t, send, recv, at):
-        pltpu.make_async_copy(
-            send.at[rows16(me.mine), cols(at)], recv.at[me.x * 2, :, cols(at)], precv.at[t]
-        ).start()
+    def spread(t, send, recv, at, early=False):
+        sem = precv.at[3 if early else t]
+        pltpu.make_async_copy(send.at[rows16(me.mine), cols(at)], recv.at[me.x * 2, :, cols(at)], sem).start()
         for i, j in NEAR:
             x, e, device = me.peer(i, j)
             remote(
-                send.at[rows16(e), cols(at)], recv.at[me.x * 2 + j, :, cols(at)], psend.at[t], precv.at[t], device
+                send.at[rows16(e), cols(at)], recv.at[me.x * 2 + j, :, cols(at)], psend.at[t], sem, device
             ).start()
 
     def spread_back(t, send, recv, at, sem):
@@ -242,37 +241,38 @@
     def norm_rows(t, s):
         at, n = sets[s]
         rows = pl.ds(at, n)
-        stat[0, rows] = jnp.zeros((n, 1), jnp.float32)
-        stat[1, rows] = jnp.zeros((n, 1), jnp.float32)
-        hidden[rows] = jnp.zeros((n, HID), jnp.float32)
+        hid, st = (hidden, stat) if t else (hidden_a, stat_a)
+        st[0, rows] = jnp.zeros((n, 1), jnp.float32)
+        st[1, rows] = jnp.zeros((n, 1), jnp.float32)
+        hid[rows] = jnp.zeros((n, HID), jnp.float32)
 
         @pl.loop(0, PARTS)
         def _(q):
             x = rows_of(t, s, q).astype(jnp.float32)
-            stat[0, rows] += jnp.sum(x * x, axis=1, keepdims=True)
-
-        stat[0, rows] = lax.rsqrt(stat[0, rows] / D + EPS)
+            st[0, rows] += jnp.sum(x * x, axis=1, keepdims=True)
+
+        st[0, rows] = lax.rsqrt(st[0, rows] / D + EPS)
 
         @pl.loop(0, PARTS)
         def _(q):
-            normed = (rows_of(t, s, q).astype(jnp.float32) * stat[0, rows]).astype(BF)
+            normed = (rows_of(t, s, q).astype(jnp.float32) * st[0, rows]).astype(BF)
             put_rows(t, s, q, normed)
-            hidden[rows] += dot(normed, up[part_rows(q)])
-            stat[1, rows] += jnp.sum(normed.astype(jnp.float32) * column[0:1, cols(q)], axis=1, keepdims=True)
-
-        stat[2, rows] = jax.nn.sigmoid(stat[1, rows])
+            hid[rows] += dot(normed, up[part_rows(q)])
+            st[1, rows] += jnp.sum(normed.astype(jnp.float32) * column[0:1, cols(q)], axis=1, keepdims=True)
+
+        st[2, rows] = jax.nn.sigmoid(st[1, rows])
 
     def forward_rows(s):
         at, n = sets[s]
         rows = pl.ds(at, n)
         norm_rows(0, s)
-        h = hidden[rows]
+        h = hidden_a[rows]
         act_a[rows] = (h * jax.nn.sigmoid(h)).astype(BF)
 
     def out_rows(s, q):
         at, n = sets[s]
         rows = pl.ds(at, n)
-        value = (stat[2, rows] * dot(act_a[rows], down[:, cols(q)])).astype(BF)
+        value = (stat_a[2, rows] * dot(act_a[rows], down[:, cols(q)])).astype(BF)
         if s < 2:
             put(ret_a, PARTS * s + q, value)
         else:
@@ -310,18 +310,21 @@
         else:
             tail_ret[:, cols(q)] = value.astype(BF)
 
-    def far_copy(t, out, to, q):
+    def far_copy(t, to, q):
         return remote(
-            far.at[t, :, cols(q)], out.at[1, :, cols(q)], fsend.at[t, 1, q], frecv.at[t, 1, q], (to, me.across)
+            far.at[t, :, cols(q)], fin.at[t, 1, :, cols(q)], fsend.at[t, 1, q], frecv.at[t, 1, q], (to, me.across)
         )
 
-    def own_copy(t, out, to, q):
+    def own_copy(t, to, q):
         return remote(
-            own.at[t, :, cols(q)], out.at[0, :, cols(q)], fsend.at[t, 0, q], frecv.at[t, 0, q], (to, me.expert)
+            own.at[t, :, cols(q)], fin.at[t, 0, :, cols(q)], fsend.at[t, 0, q], frecv.at[t, 0, q], (to, me.expert)
         )
 
-    def own_stay(t, out, q):
-        return pltpu.make_async_copy(own.at[t, :, cols(q)], out.at[0, :, cols(q)], frecv.at[t, 0, q])
+    def own_stay(t, q):
+        return pltpu.make_async_copy(own.at[t, :, cols(q)], fin.at[t, 0, :, cols(q)], frecv.at[t, 0, q])
+
+    def out_copy(t, out, q):
+        return pltpu.make_async_copy(fin.at[t, 0, :, cols(q)], out.at[:, cols(q)], out_sem.at[t, q])
 
     ends = ((ga, own_a, oa, a_to), (gb, got_b.at[2], ob, b_to))
 
@@ -333,37 +336,37 @@
         arrived(recv.at[:, :, pl.ds(0, 2 * W)], grecv.at[t, q])
         second = block(recv, PARTS + q)
         far[t, :, cols(q)] = (dot(sums[t, 2], second) + dot(sums[t, 3 + q], block(recv, 2 * PARTS))).astype(BF)
-        far_copy(t, out, to, q).start()
+        far_copy(t, to, q).start()
         own[t, :, cols(q)] = (
             base[:, cols(q)].astype(jnp.float32) + dot(sums[t, 0], block(recv, q)) + dot(sums[t, 1], second)
         ).astype(BF)
         if t == 0:
-            own_copy(t, out, to, q).start()
+            own_copy(t, to, q).start()
         else:
             @pl.when(stays)
             def _():
-                own_stay(t, out, q).start()
+                own_stay(t, q).start()
 
             @pl.when(jnp.logical_not(stays))
             def _():
-                own_copy(t, out, to, q).start()
+                own_copy(t, to, q).start()
 
     def down_part(at, q):
         total = 0.0
         for s, (first, n) in enumerate(sets):
             total += dot_tn(act[pl.ds(first, n), pl.ds(at, HALF)], rows_of(2, s, q))
-        return total.astype(BF)
+        return total
 
     def up_part(at, q):
         total = 0.0
         for s, (first, n) in enumerate(sets):
             total += dot_tn(rows_of(1, s, q), hid_grad[pl.ds(first, n), pl.ds(at, HALF)])
-        return total.astype(BF)
+        return total
 
     def grad_copies(q):
         return [
-            remote(down_far.at[:, cols(q)], down_out.at[1, :, cols(q)], dsend.at[0, q], drecv.at[0, q], me.twin),
-            remote(up_far.at[part_rows(q)], up_out.at[1, part_rows(q)], dsend.at[1, q], drecv.at[1, q], me.twin),
+            remote(down_far.at[:, cols(q)], down_got.at[:, cols(q)], dsend.at[0, q], drecv.at[0, q], me.twin),
+            remote(up_far.at[part_rows(q)], up_got.at[part_rows(q)], dsend.at[1, q], drecv.at[1, q], me.twin),
         ]
 
     a_row, a_col = codes_of(a_ids[...])
@@ -373,7 +376,7 @@
     @pl.loop(0, PARTS)
     def _(q):
         send_a[:, cols(q)] = dot(sel[0, 0], own_a[:, cols(q)]).astype(BF)
-        spread(0, send_a, ra, q)
+        spread(0, send_a, ra, q, early=True)
 
     for copy in small:
         copy.wait()
@@ -381,35 +384,50 @@
     b_far_row, b_far_col = codes_of(ids[2])
     fill_selectors(selector, sel, 1, b_row, b_far_row)
 
-    for t, send, recv in ((1, send_bx, rbx), (2, send_bc, rbc)):
-        left[...] = jnp.zeros_like(left)
-
-        @pl.loop(0, PARTS)
-        def _(q):
-            z_copy(2 * t - 1, q).wait()
-            here = got_b[2 * t - 2, :, cols(q)]
-            send[:, cols(q)] = dot(sel[1, 0], here).astype(BF)
-            spread(t, send, recv, q)
-            z_copy(2 * t, q).wait()
-            there = got_b[2 * t - 1, :, cols(q)]
-            send[:, cols(PARTS + q)] = (dot(sel[1, 1], here) + dot(sel[1, 2], there)).astype(BF)
-            left[...] += dot(sel[1, 3 + q], there)
-            spread(t, send, recv, PARTS + q)
-
+    def slot_part(t, send, recv, q):
+        z_copy(2 * t - 1, q).wait()
+        here = got_b[2 * t - 2, :, cols(q)]
+        send[:, cols(q)] = dot(sel[1, 0], here).astype(BF)
+        spread(t, send, recv, q)
+        z_copy(2 * t, q).wait()
+        there = got_b[2 * t - 1, :, cols(q)]
+        send[:, cols(PARTS + q)] = (dot(sel[1, 1], here) + dot(sel[1, 2], there)).astype(BF)
+        left[...] += dot(sel[1, 3 + q], there)
+        spread(t, send, recv, PARTS + q)
+
+    def slot_tail(t, send, recv):
         send[:, 2 * D:] = left[...].astype(BF)
         spread(t, send, recv, 2 * PARTS)
-        if t == 1:
-            a_far_row, a_far_col = codes_of(ids[0])
-            fill_selectors(selector, sel, 0, a_row, a_far_row)
-            fill_selectors(unselector, sums, 0, a_col, a_far_col)
-            fill_selectors(unselector, sums, 1, b_col, b_far_col)
-
-    for copy in loads[1:] + weights:
-        copy.wait()
-    arrived(rbx, precv.at[1])
-    pick_tail(1)
-    for s in (2, 0, 1):
-        norm_rows(1, s)
+        left[...] = jnp.zeros_like(left)
+
+    left[...] = jnp.zeros_like(left)
+
+    @pl.loop(0, PARTS)
+    def _(q):
+        slot_part(1, send_bx, rbx, q)
+
+    slot_tail(1, send_bx, rbx)
+    a_far_row, a_far_col = codes_of(ids[0])
+    fill_selectors(selector, sel, 0, a_row, a_far_row)
+    fill_selectors(unselector, sums, 0, a_col, a_far_col)
+    fill_selectors(unselector, sums, 1, b_col, b_far_col)
+
+    for q in range(PARTS):
+        slot_part(2, send_bc, rbc, q)
+        if q == 1:
+            loads[1].wait()
+            weights[0].wait()
+            arrived(rbx, precv.at[1])
+            pick_tail(1)
+            for s in (2, 0, 1):
+                norm_rows(1, s)
+        if q == 2:
+            arrived(ra.at[:, :, pl.ds(0, D)], precv.at[3])
+            forward_rows(0)
+    slot_tail(2, send_bc, rbc)
+
+    loads[2].wait()
+    weights[1].wait()
     arrived(rbc, precv.at[2])
     pick_tail(2)
     for s in (2, 0, 1):
@@ -431,16 +449,18 @@
 
     @pl.loop(0, PARTS)
     def _(q):
-        down_far[:, cols(q)] = down_part(HALF, q)
-        up_far[part_rows(q)] = up_part(HALF, q)
+        down_far[:, cols(q)] = down_part(HALF, q).astype(BF)
+        up_far[part_rows(q)] = up_part(HALF, q).astype(BF)
         for copy in grad_copies(q):
             copy.start()
 
-    left[...] = jnp.zeros_like(left)
-    for q in range(PARTS):
-        if q == PARTS - 1:
-            collect_edge(1)
-            collect(1, 0)
+    @pl.loop(0, PARTS)
+    def _(q):
+        out_rows(0, q)
+        spread_back(0, ret_a, ga, q, q)
+
+    @pl.loop(0, PARTS)
+    def _(q):
         z_copy(0, q).wait()
         there = far_a[:, cols(q)]
         send_a[:, cols(PARTS + q)] = (dot(sel[0, 1], own_a[:, cols(q)]) + dot(sel[0, 2], there)).astype(BF)
@@ -450,11 +470,13 @@
     send_a[:, 2 * D:] = left[...].astype(BF)
     spread(0, send_a, ra, 2 * PARTS)
 
-    @pl.loop(1, PARTS)
+    collect_edge(1)
+
+    @pl.loop(0, PARTS)
     def _(q):
         collect(1, q)
 
-    arrived(ra, precv.at[0])
+    arrived(ra.at[:, :, pl.ds(D, D + W)], precv.at[0])
     pick_tail(0)
     forward_rows(2)
 
@@ -465,32 +487,52 @@
     put_tail(ret_a)
     spread_back(0, ret_a, ga, 2 * PARTS, PARTS)
     forward_rows(1)
-    forward_rows(0)
 
     @pl.loop(0, PARTS)
     def _(q):
         out_rows(1, q)
         spread_back(0, ret_a, ga, PARTS + q, q)
-        out_rows(0, q)
-        spread_back(0, ret_a, ga, q, q)
-
-    @pl.loop(0, PARTS)
-    def _(q):
-        down_own[:, cols(q)] = down_part(0, q)
-        up_own[part_rows(q)] = up_part(0, q)
+
+    collect_edge(0)
+
+    @pl.loop(0, PARTS)
+    def _(q):
+        collect(0, q)
+
+    @pl.loop(0, PARTS)
+    def _(q):
+        for copy in grad_copies(q):
+            copy.wait()
+        down_got[:, cols(q)] = (down_got[:, cols(q)].astype(jnp.float32) + down_part(0, q)).astype(BF)
+        up_got[part_rows(q)] = (up_got[part_rows(q)].astype(jnp.float32) + up_part(0, q)).astype(BF)
 
     stores = [
-        pltpu.make_async_copy(up_own, up_out.at[0], local.at[3]),
-        pltpu.make_async_copy(down_own, down_out.at[0], local.at[4]),
+        pltpu.make_async_copy(up_got, up_out, local.at[3]),
+        pltpu.make_async_copy(down_got, down_out, local.at[4]),
     ]
     for copy in stores:
         copy.start()
 
-    collect_edge(0)
-
-    @pl.loop(0, PARTS)
-    def _(q):
-        collect(0, q)
+    for t in (1, 0):
+        recv, base, out, to = ends[t]
+
+        @pl.loop(0, PARTS)
+        def _(q):
+            if t == 0:
+                own_copy(t, to, q).wait()
+            else:
+                @pl.when(jnp.logical_not(stays))
+                def _():
+                    own_copy(t, to, q).wait()
+
+                @pl.when(stays)
+                def _():
+                    own_stay(t, q).wait()
+            far_copy(t, to, q).wait()
+            fin[t, 0, :, cols(q)] = (
+                fin[t, 0, :, cols(q)].astype(jnp.float32) + fin[t, 1, :, cols(q)].astype(jnp.float32)
+            ).astype(BF)
+            out_copy(t, out, q).start()
 
     for t, recv in enumerate(recvs):
         most = recv.at[pl.ds(0, GROUP - 1)]
@@ -501,19 +543,7 @@
 
         @pl.loop(0, PARTS)
         def _(q):
-            far_copy(t, out, to, q).wait()
-            if t == 0:
-                own_copy(t, out, to, q).wait()
-                for copy in grad_copies(q):
-                    copy.wait()
-            else:
-                @pl.when(jnp.logical_not(stays))
-                def _():
-                    own_copy(t, out, to, q).wait()
-
-                @pl.when(stays)
-                def _():
-                    own_stay(t, out, q).wait()
+            out_copy(t, out, q).wait()
     for copy in stores:
         copy.wait()
 
@@ -522,7 +552,7 @@
     anywhere = pl.BlockSpec(memory_space=pl.ANY)
     inside = pl.BlockSpec(memory_space=pltpu.VMEM)
     dma = pltpu.SemaphoreType.DMA
-    pair = jax.ShapeDtypeStruct((2, TOK, D), BF)
+    rows = jax.ShapeDtypeStruct((TOK, D), BF)
 
     def held(*shape, kind=BF):
         return pltpu.VMEM(shape, kind)
@@ -534,29 +564,26 @@
         span_kernel,
         name="span",
         out_shape=(
-            pair, pair, jax.ShapeDtypeStruct((2, D, HALF), BF), jax.ShapeDtypeStruct((2, HALF, D), BF)
+            rows, rows, jax.ShapeDtypeStruct((D, HALF), BF), jax.ShapeDtypeStruct((HALF, D), BF)
         ),
         in_specs=[anywhere] * 3 + [inside] * 2 + [anywhere] * 2 + [inside],
         out_specs=(anywhere,) * 4,
         scratch_shapes=[
             held(TOK, D), held(TOK, D), held(4, TOK, D), held(3, 1, TOK, kind=jnp.int32),
             held(TOK, WIDE), held(TOK, WIDE), held(TOK, WIDE), *[block_of() for _ in range(7)],
-            held(2, TOK, D), held(2, TOK, D), held(D, HID), held(HID, D),
+            held(2, TOK, D), held(2, TOK, D), held(2, 2, TOK, D), held(D, HID), held(HID, D),
             held(D, HALF), held(D, HALF), held(HALF, D), held(HALF, D),
             held(TOK, W, kind=jnp.float32), held(2, 3 + PARTS, TOK, TOK), held(2, 3 + PARTS, TOK, LINES),
             held(3, TAIL, D), held(TAIL, D),
-            held(ROWS, HID, kind=jnp.float32), held(ROWS, HID, kind=jnp.float32),
-            held(ROWS, HID), held(ROWS, HID), held(ROWS, HID), held(5, ROWS, 1, kind=jnp.float32),
-            dma((5, PARTS)), dma((5, PARTS)), dma((3,)), dma((3,)), dma((3,)), dma((3,)),
+            *[held(ROWS, HID, kind=jnp.float32) for _ in range(3)],
+            held(ROWS, HID), held(ROWS, HID), held(ROWS, HID),
+            held(5, ROWS, 1, kind=jnp.float32), held(3, ROWS, 1, kind=jnp.float32),
+            dma((5, PARTS)), dma((5, PARTS)), dma((3,)), dma((3,)), dma((3,)), dma((4,)),
             dma((2,)), dma((2, PARTS + 1)), dma((2, 2, PARTS)), dma((2, 2, PARTS)),
-            dma((2,)), dma((2,)), dma((2, PARTS)), dma((2, PARTS)), dma((5,)),
+            dma((2,)), dma((2,)), dma((2, PARTS)), dma((2, PARTS)), dma((2, PARTS)), dma((5,)),
         ],
         compiler_params=pltpu.CompilerParams(collective_id=1, has_side_effects=True, vmem_limit_bytes=67043328),
     )(*operands)
-
-
-def add_pair(pair):
-    return (pair[0].astype(jnp.float32) + pair[1].astype(jnp.float32)).astype(BF)[None]
 
 
 def body(a_input, a_route, b_saved, b_grad, b_route, up_weight, down_weight, router):
@@ -567,7 +594,7 @@
         a_input[0], b_saved[0], b_grad[0], a_route.reshape(1, TOK), b_route.reshape(1, TOK),
         up_weight[0], down_weight[0], column,
     )
-    return add_pair(out_a), add_pair(out_b), add_pair(up_grad), add_pair(down_grad)
+    return out_a[None], out_b[None], up_grad[None], down_grad[None]
 
 
 def solution(mesh):

time: 237 us -> 239 us (level)
  the two profiles are of different devices: /device:TPU:33 before, /device:TPU:92 now
where the time goes in v4:
time: 239 us; the launch traced here: 235 us
  Pallas kernels  226 us (95%)
  local copies, waits for them, and re-layouts  6.63 us (3%)
    pallas_call x1, Pallas kernels, span(): pl.pallas_call(span_kernel, name='span', out_shape=(rows, rows, jax.Shape...  226 us
    unnamed x10, local copies, waits for them, and re-layouts  6.63 us

profile of v4, /device:TPU:92, one launch (start us, length us, event | category | flops | bytes accessed | tf_op | source)
XLA Modules:
  0.0 234.8 jit_solution(1804140933025231298)
XLA Ops:
  0.6 1.4 bitcast_convert_fusion.column
  2.1 226.0 %span.1 = (bf16[128,3584]{1,0:T(8,128)(2,1)}, bf16[128,3584]{1,0:T(8,128)(2,1)}, bf16[3584,256]{1,0:T(8,128)(2,1)}, bf16[256,3584]{1,0:T(8,128)(2,1)}) custom-call(bf16[128,3584]{1,0:T(8,128)(2,1)} %bitcast.20, bf16[128,3584]{1,0:T(8,128)(2,1)} %bitcast.21, bf16[128,3584]{1,0:T(8,128)(2,1)} %bitcast.22, s32[1,128]{1,0:T(1,128)} %bitcast.23, ...), custom_call_target="tpu_custom_call" | custom-call | tf_op jit(solution)/shard_map/span/pallas_call | solution.py:563
  228.1 0.0 copy-start.2
  228.1 0.0 copy-start.1
  228.1 2.3 copy.16
  230.4 0.0 copy-done.2
  230.4 0.9 copy.17
  231.4 0.0 copy-done.1
  231.4 0.0 copy-start
  231.4 1.2 copy.18
  232.6 0.9 copy-done
  233.5 1.2 copy.19
Async XLA Ops:
  228.1 2.3 copy-start.2
  228.1 3.2 %copy-start.1 = (bf16[3584,256]{1,0:T(8,128)(2,1)S(1)}, bf16[3584,256]{1,0:T(8,128)(2,1)}, u32[]{:S(2)}) copy-start(bf16[3584,256]{1,0:T(8,128)(2,1)} %get-tuple-element.10) | copy-start | bytes 5505028
  231.4 2.2 copy-start
